TPU v7x, 256 devices: a whole 4x4x8 slice. The times are simulated.
256 devices in a mesh: section: 4 (over y_lo, core), seq: 16 (over y_hi, z), expert: 4 (over x).
Axes of the slice: x: 4, y: 4 (y_hi: 2, y_lo: 2; y = y_hi * 2 + y_lo), z: 8, core: 2. Of those that a mesh axis runs over, the one named last changes fastest.
Arguments:
- queries: bfloat16 [16, 1536, 4096], P(('section', 'expert'), 'seq'), may hold values from -112 to 112
- dec_state: bfloat16 [16, 1536, 4096], P(('section', 'expert'), 'seq'), may hold values from -6 to 6
- enc_kv: bfloat16 [2, 16, 2560, 1024], P(None, ('section', 'expert'), 'seq'), may hold values from -15 to 15
- band_start: int32 [16, 16], P(('section', 'expert'), 'seq'), may hold values from 0 to 2432, as said below
- norm_gain: float32 [4096], replicated, may hold values from 0.5 to 1.5
- route_ids: int32 [16, 1536, 1], P(('section', 'expert'), 'seq'), may hold values from 0 to 31; in each aligned block of 96 rows (0 to 95, 96 to 191, ..., all dimensions but the last counted through in order) at most 3 rows name the same one
- keep: int32 [16, 1536], P(('section', 'expert'), 'seq'), may hold values 0 or 1
- route_prob: float32 [16, 1536], P(('section', 'expert'), 'seq'), may hold values from 0.25 to 1
- w_in: bfloat16 [32, 5120, 4096], P('seq', ('section', 'expert')), may hold values from -0.09375 to 0.09375
- w_out: bfloat16 [32, 5120, 4096], P('seq', ('section', 'expert')), may hold values from -0.078125 to 0.078125
Outputs:
- mixed: bfloat16 [16, 1536, 4096], P(('section', 'expert'), 'seq')
Inputs may be any that keep to these rules, and one draw needn't show every extreme that they name: `band_start`: block q's band lies within encoder frames (q - 1) * 160 to (q + 2) * 160 - 1. `route_ids`: among the tokens of one device no expert is named more than 3 times.
All inputs are finite; a program needn't handle non-finite values. No bound on the sum of `keep` on one device may be relied on, other than what follows from the above.
Results may differ from a plain program's by a relative error of at most 0.011.
Values may be sent and summed in bfloat16 or wider, within the bound.
A program may use at most 128 MiB of HBM per device.

v0:
```python
import math

import jax
import jax.numpy as jnp
from jax import lax
from jax.sharding import PartitionSpec as P

D = 4096
HEADS = 32
KV_HEADS = 8
DH = 128
WIN = 128


def shifted(block, axis, distance):
    devices = range(lax.axis_size(axis))
    route = [((i - distance) % len(devices), i) for i in devices]
    return lax.ppermute(block, axis, route)


def extended(cells, sides, width):
    for axis, dim in sides:
        count = lax.axis_size(axis)
        ends = count - 1
        head = lax.slice_in_dim(cells, 0, width, axis=dim)
        tail = lax.slice_in_dim(cells, cells.shape[dim] - width, cells.shape[dim], axis=dim)
        cells = jnp.concatenate(
            [
                lax.ppermute(tail, axis, [(i, (i + 1) % count) for i in range(ends)]),
                cells,
                lax.ppermute(head, axis, [((i + 1) % count, i) for i in range(ends)]),
            ],
            axis=dim,
        )
    return cells


def cross_attend(query_rows, band_pair):
    tok_count = query_rows.shape[0]
    groups = HEADS // KV_HEADS
    grouped = query_rows.reshape(tok_count, KV_HEADS, groups, DH)
    keys_b = band_pair[0].reshape(WIN, KV_HEADS, DH)
    values_b = band_pair[1].reshape(WIN, KV_HEADS, DH)
    scores = jnp.einsum(
        "tkgd,wkd->kgtw", grouped, keys_b, preferred_element_type=jnp.float32
    ) / math.sqrt(DH)
    row_peak = jnp.max(scores, axis=-1, keepdims=True)
    weights = jnp.exp(scores - row_peak)
    row_total = jnp.sum(weights, axis=-1)
    rounded = weights.astype(jnp.bfloat16)
    context = jnp.einsum("kgtw,wkd->tkgd", rounded, values_b, preferred_element_type=jnp.float32)
    context = context / jnp.transpose(row_total, (2, 0, 1))[..., None]
    return context.reshape(tok_count, HEADS * DH)


def body(
    queries, dec_state, enc_kv, band_start, norm_gain, route_ids, keep, route_prob, w_in, w_out
):
    own_pair = shifted(enc_kv[:, 0], "section", 1)
    frames_dev = own_pair.shape[1]
    offset = band_start[0, 0]
    position = lax.axis_index("seq")
    widened = extended(own_pair, (("seq", 1),), frames_dev)
    local_first = offset - (position - 1) * frames_dev
    band_pair = lax.dynamic_slice_in_dim(widened, local_first, WIN, 1)
    context = cross_attend(queries[0], band_pair)
    state = dec_state[0].astype(jnp.float32) + context
    normed = (
        state * lax.rsqrt(jnp.mean(state * state, axis=-1, keepdims=True) + 1e-06) * norm_gain
    ).astype(jnp.bfloat16)
    experts_of = route_ids[0, :, 0]
    tok_count = experts_of.shape[0]
    seq_count = lax.axis_size("seq")
    per_device = w_in.shape[0]
    expert_count = per_device * seq_count
    capacity = max(2, tok_count // expert_count)
    one_hot = (experts_of[:, None] == jnp.arange(expert_count, dtype=jnp.int32)[None, :]).astype(
        jnp.int32
    )
    earlier = jnp.cumsum(one_hot, axis=0) - one_hot
    slot_of = jnp.sum(earlier * one_hot, axis=1)
    target = experts_of * capacity + slot_of
    kept = keep[0] == 1
    slot_ids = jnp.arange(expert_count * capacity, dtype=jnp.int32)
    dispatch = ((slot_ids[:, None] == target[None, :]) & kept[None, :]).astype(jnp.bfloat16)
    outgoing = jnp.dot(dispatch, normed, preferred_element_type=jnp.float32).astype(jnp.bfloat16)
    outgoing = outgoing.reshape(seq_count, per_device, capacity, D)
    arrived = lax.all_to_all(outgoing, "seq", split_axis=0, concat_axis=2, tiled=True)[0]
    hidden = jnp.einsum(
        "emd,efd->emf",
        lax.all_gather(arrived, ("section", "expert"), axis=1, tiled=True),
        w_in,
        preferred_element_type=jnp.float32,
    )
    hidden = jnp.maximum(hidden, 0.0).astype(jnp.bfloat16)
    partials = jnp.einsum("emf,efd->emd", hidden, w_out, preferred_element_type=jnp.float32)
    summed = lax.psum_scatter(
        partials.astype(jnp.bfloat16), ("section", "expert"), scatter_dimension=1, tiled=True
    )
    returned = lax.all_to_all(summed, "seq", split_axis=1, concat_axis=0, tiled=True).reshape(
        expert_count * capacity, D
    )
    expert_out = jnp.einsum("st,sd->td", dispatch, returned, preferred_element_type=jnp.float32)
    scale = (keep[0].astype(jnp.float32) * route_prob[0])[:, None]
    return (state + scale * expert_out).astype(jnp.bfloat16)[None]


def solution(mesh):
    return jax.shard_map(
        body,
        mesh=mesh,
        in_specs=(
            P(("section", "expert"), "seq", None),
            P(("section", "expert"), "seq", None),
            P(None, ("section", "expert"), "seq", None),
            P(("section", "expert"), "seq"),
            P(),
            P(("section", "expert"), "seq", None),
            P(("section", "expert"), "seq"),
            P(("section", "expert"), "seq"),
            P("seq", ("section", "expert"), None),
            P("seq", ("section", "expert"), None),
        ),
        out_specs=P(("section", "expert"), "seq", None),
        check_vma=False,
    )
```

profile of v0, /device:TPU:1, one launch (start us, length us, event | category | flops | bytes accessed | tf_op | source)
XLA Modules:
  0.0 385.2 jit_solution(8837927128330509526)
XLA Ops:
  6.5 0.0 all-gather.2.cloned.1.call-start
  6.5 2.7 collective-permute-start
  9.2 7.8 %collective-permute-done = bf16[2,160,1024]{2,1,0:T(8,128)(2,1)S(1)} collective-permute-done((bf16[2,160,1024]{2,1,0:T(8,128)(2,1)}, bf16[2,160,1024]{2,1,0:T(8,128)(2,1)S(1)}, u32[]{:S(2)}, u32[]{:S(2)}) %collective-permute-start) | collective-permute-done | bytes 655392 | tf_op jit(solution)/shard_map/ppermute | solution.py:18
  17.1 4.4 %collective-permute-start.1 = (bf16[2,160,1024]{2,1,0:T(8,128)(2,1)S(1)}, bf16[2,160,1024]{2,1,0:T(8,128)(2,1)}, u32[]{:S(2)}, u32[]{:S(2)}) collective-permute-start(bf16[2,160,1024]{2,1,0:T(8,128)(2,1)S(1)} %collective-permute-done), channel_id=1, source_target_pairs={{0,4},{4,8},{8,12},{12,16},{16,20},{20,24},{24,28},{28,32},{32,36}... | collective-permute-start | bytes 1966088 | tf_op jit(solution)/shard_map/ppermute | solution.py:29
  21.5 1.3 collective-permute-start.2
  22.7 0.7 fusion.20
  24.1 3.0 reshape_squeeze.11
  27.1 0.0 copy-done
  27.1 2.3 reshape.52
  29.5 0.1 reduce_window_sum.11
  29.6 0.0 copy-done.5
  29.6 0.2 select_reduce_fusion
  29.8 0.0 copy-done.6
  29.8 0.5 copy.22
  30.3 3.1 collective-permute-done.1
  33.4 1.4 copy.21
  34.8 3.4 collective-permute-done.2
  38.2 2.2 copy.23
  40.4 2.3 fusion.19
  42.7 0.0 copy-done.2
  42.7 0.0 copy-start.3
  42.8 0.8 bitcast_reduce_fusion
  43.6 1.1 fusion.10
  44.6 0.0 copy-done.3
  44.6 2.2 fusion.9
  46.9 2.2 copy.27
  49.1 1.9 reshape.48
  51.0 0.0 copy-done.4
  51.0 1.4 convolution_convert_fusion.1
  52.4 1.5 reshape.49
  53.9 1.0 copy.29
  54.8 27.7 %all_to_all.30 = bf16[16,2,3,4096]{3,1,2,0:T(2,128)(2,1)} all-to-all(bf16[16,2,3,4096]{3,1,2,0:T(2,128)(2,1)S(1)} %copy.29), channel_id=1, replica_groups=mesh['section'=4,'seq'=16,'expert'=4] {'seq'}, dimensions={0} | all-to-all | bytes 1572864 | tf_op jit(solution)/shard_map/all_to_all | solution.py:88
  82.5 0.0 all-gather.2.cloned.1.call-update
  82.6 0.2 reduce-scatter.2.cloned.1.call-start
  82.8 78.8 %all-gather.2.cloned.1.call-done = bf16[2,768,4096]{2,0,1:T(2,128)(2,1)} async-done(((bf16[2,48,4096]{2,0,1:T(2,128)(2,1)}), bf16[2,768,4096]{2,0,1:T(2,128)(2,1)}) %all-gather.2.cloned.1.call-update) | async-done | bytes 12582928 | tf_op jit(solution)/shard_map/all_gather | solution.py:91
  161.6 22.0 %maximum_convert_fusion = bf16[2,768,320]{1,2,0:T(8,128)(2,1)S(1)} fusion(bf16[2,320,4096]{2,1,0:T(8,128)(2,1)} %param.18, bf16[2,768,4096]{2,0,1:T(2,128)(2,1)} %all-gather.2.cloned.1.call-done), kind=kOutput, calls=%fused_computation.11 | convolution fusion | flops 4027514880 | bytes 18808832 | tf_op jit(solution)/shard_map/emd,efd->emf/dot_general | solution.py:89
  183.6 12.1 %convolution_convert_fusion = bf16[2,768,4096]{2,1,0:T(8,128)(2,1)} fusion(bf16[2,768,320]{1,2,0:T(8,128)(2,1)S(1)} %maximum_convert_fusion, bf16[2,320,4096]{2,1,0:T(8,128)(2,1)} %param.19), kind=kOutput, calls=%fused_computation.2 | convolution fusion | flops 4032823296 | bytes 18808832 | tf_op jit(solution)/shard_map/emf,efd->emd/dot_general | solution.py:96
  195.7 0.0 reduce-scatter.2.cloned.1.call-update
  195.8 0.0 copy-start.7
  195.8 142.8 %reduce-scatter.2.cloned.1.call-done = bf16[2,48,4096]{2,1,0:T(8,128)(2,1)} async-done(((bf16[2,768,4096]{2,1,0:T(8,128)(2,1)}), bf16[2,48,4096]{2,1,0:T(8,128)(2,1)}) %reduce-scatter.2.cloned.1.call-update) | async-done | bytes 786448 | tf_op jit(solution)/shard_map/reduce_scatter | solution.py:97
  338.6 2.8 copy.31
  341.4 9.3 %all-to-all-start.1 = ((bf16[2,48,4096]{2,0,1:T(2,128)(2,1)}), bf16[2,48,4096]{2,0,1:T(2,128)(2,1)S(1)}, u32[]{:S(2)}, u32[]{:S(2)}) async-start(bf16[2,48,4096]{2,0,1:T(2,128)(2,1)} %copy.31), calls=%async_computation.2 | async-start | bytes 1572864 | tf_op jit(solution)/shard_map/all_to_all | solution.py:100
  350.7 0.0 copy-done.7
  350.7 21.0 %all-to-all-done.1 = bf16[2,48,4096]{2,0,1:T(2,128)(2,1)S(1)} async-done(((bf16[2,48,4096]{2,0,1:T(2,128)(2,1)}), bf16[2,48,4096]{2,0,1:T(2,128)(2,1)S(1)}, u32[]{:S(2)}, u32[]{:S(2)}) %all-to-all-start.1) | async-done | bytes 786464 | tf_op jit(solution)/shard_map/all_to_all | solution.py:100
  371.7 0.9 copy-done.1
  372.6 1.8 copy.32
  374.4 1.4 reshape.50
  375.9 2.5 fusion.4
  (11 shorter events, 0.1 us)
Async XLA Ops:
  6.5 20.6 %copy-start = (bf16[1,96,4096]{2,1,0:T(8,128)(2,1)S(1)}, bf16[1,96,4096]{2,1,0:T(8,128)(2,1)}, u32[]{:S(2)}) copy-start(bf16[1,96,4096]{2,1,0:T(8,128)(2,1)} %param.11) | copy-start | bytes 2359300
  6.5 155.0 %all-gather.2.cloned.1.call-start = ((), (), s32[]{:S(2)}) async-start(), calls=%async_computation.3 | async-start | bytes 13369344 | tf_op jit(solution)/shard_map/all_gather | solution.py:91
  6.5 10.5 %collective-permute-start = (bf16[2,160,1024]{2,1,0:T(8,128)(2,1)}, bf16[2,160,1024]{2,1,0:T(8,128)(2,1)S(1)}, u32[]{:S(2)}, u32[]{:S(2)}) collective-permute-start(bf16[2,160,1024]{2,1,0:T(8,128)(2,1)} %bitcast.64), channel_id=1, source_target_pairs={{192,0},{0,64},{64,128},{128,192},{193,1},{1,65},{65,129},{129,193... | collective-permute-start | bytes 1966088 | tf_op jit(solution)/shard_map/ppermute | solution.py:18
  17.1 16.4 %collective-permute-start.1 = (bf16[2,160,1024]{2,1,0:T(8,128)(2,1)S(1)}, bf16[2,160,1024]{2,1,0:T(8,128)(2,1)}, u32[]{:S(2)}, u32[]{:S(2)}) collective-permute-start(bf16[2,160,1024]{2,1,0:T(8,128)(2,1)S(1)} %collective-permute-done), channel_id=1, source_target_pairs={{0,4},{4,8},{8,12},{12,16},{16,20},{20,24},{24,28},{28,32},{32,36}... | collective-permute-start | bytes 1966088 | tf_op jit(solution)/shard_map/ppermute | solution.py:29
  21.5 16.7 %collective-permute-start.2 = (bf16[2,160,1024]{2,1,0:T(8,128)(2,1)S(1)}, bf16[2,160,1024]{2,1,0:T(8,128)(2,1)}, u32[]{:S(2)}, u32[]{:S(2)}) collective-permute-start(bf16[2,160,1024]{2,1,0:T(8,128)(2,1)S(1)} %collective-permute-done), channel_id=1, source_target_pairs={{4,0},{8,4},{12,8},{16,12},{20,16},{24,20},{28,24},{32,28},{36,32}... | collective-permute-start | bytes 1966088 | tf_op jit(solution)/shard_map/ppermute | solution.py:31
  27.1 2.5 copy-start.5
  27.1 2.7 copy-start.6
  40.4 2.4 copy-start.2
  42.7 1.9 copy-start.3
  49.1 1.9 copy-start.4
  82.6 256.0 %reduce-scatter.2.cloned.1.call-start = ((), (), s32[]{:S(2)}) async-start(), calls=%async_computation.4 | async-start | bytes 13369344 | tf_op jit(solution)/shard_map/reduce_scatter | solution.py:97
  195.8 154.9 %copy-start.7 = (f32[1,96]{1,0:T(1,128)S(1)}, f32[1,96]{1,0:T(1,128)}, u32[]{:S(2)}) copy-start(f32[1,96]{1,0:T(1,128)} %param.17) | copy-start | bytes 1156
  341.4 30.3 %all-to-all-start.1 = ((bf16[2,48,4096]{2,0,1:T(2,128)(2,1)}), bf16[2,48,4096]{2,0,1:T(2,128)(2,1)S(1)}, u32[]{:S(2)}, u32[]{:S(2)}) async-start(bf16[2,48,4096]{2,0,1:T(2,128)(2,1)} %copy.31), calls=%async_computation.2 | async-start | bytes 1572864 | tf_op jit(solution)/shard_map/all_to_all | solution.py:100
  371.7 0.9 copy-start.1
Sparse Core Ops, SparseCore 0:
  82.7 78.8 all-gather.1
  195.9 142.6 reduce-scatter.1
where the time goes:
time: 386 us; the launch traced here: 385 us
  waiting for transfers between devices  257 us (67%)
  matrix products  41 us (11%)
  blocking collectives  27.7 us (7%)
  local copies, waits for them, and re-layouts  23 us (6%)
  starting transfers between devices  17.8 us (5%)
  between operations  14.2 us (4%)
  other arithmetic  4.44 us (1%)
    reduce_scatter x1, waiting for transfers between devices, body(): lax.psum_scatter(partials.astype(jnp.bfloat16), ('section', 'expert'), sc...  143 us
    all_gather x1, waiting for transfers between devices, body(): lax.all_gather(arrived, ('section', 'expert'), axis=1, tiled=True)  78.8 us
    all_to_all x1, blocking collectives, body(): lax.all_to_all(outgoing, 'seq', split_axis=0, concat_axis=2, tiled=True)[0]  27.7 us
    dot_general x1, matrix products, body(): jnp.einsum('emd,efd->emf', lax.all_gather(arrived, ('section', 'expert'),...  22 us
    all_to_all x1, waiting for transfers between devices, body(): lax.all_to_all(summed, 'seq', split_axis=1, concat_axis=0, tiled=True)  21 us
    dot_general x1, matrix products, body(): jnp.einsum('emf,efd->emd', hidden, w_out, preferred_element_type=jnp.floa...  12.1 us
    all_to_all x1, starting transfers between devices, body(): lax.all_to_all(summed, 'seq', split_axis=1, concat_axis=0, tiled=True)  9.26 us
    ppermute x1, waiting for transfers between devices, shifted(): return lax.ppermute(block, axis, route)  7.85 us
  transfers between devices with their start and end apart: 6, of which 6 were waited for; matrix products, arithmetic and copies ran while one was open for 2% of the time, Pallas kernels for 0%

commit v1 on v0

--- a/solution.py
+++ b/solution.py
@@ -2,7 +2,10 @@
 
 import jax
 import jax.numpy as jnp
+import numpy as np
 from jax import lax
+from jax.experimental import pallas as pl
+from jax.experimental.pallas import tpu as pltpu
 from jax.sharding import PartitionSpec as P
 
 D = 4096
@@ -10,6 +13,21 @@
 KV_HEADS = 8
 DH = 128
 WIN = 128
+MESH = pl.DeviceIdType.MESH
+
+TOK = 96
+HALF = 48
+SEGS = 8
+SEG = D // SEGS
+MSG = 24
+PEERS = 16
+FS = 320
+PA = (0, 1152)
+PB = (1152, 1152)
+QA = (2304, 896)
+QB = (3200, 896)
+PP = (0, 2304)
+QQ = (2304, 1792)
 
 
 def shifted(block, axis, distance):
@@ -53,6 +71,450 @@
     return context.reshape(tok_count, HEADS * DH)
 
 
+def message_order():
+    order = np.zeros((SEGS * HALF, SEGS * HALF), np.float32)
+    for seg in range(SEGS):
+        for peer in range(PEERS):
+            for j in range(3):
+                order[seg * HALF + peer * 3 + j, peer * MSG + seg * 3 + j] = 1.0
+    return order
+
+
+def moe_kernel(
+    unpack_ref, pack_ref, normed_ref, state_ref, ids_col_ref, ids_row_ref, scale_ref, w_in_hbm, w_out_hbm,
+    out_ref,
+    win, wout, hid, xg, pt, out_msg, in_msg, ret_msg, ret_in, fin,
+    r_p2r, r_p2l, r_pr, r_pl, r_py, r_qy, r_q2r, r_q2l, r_qr, r_ql,
+    w_sem, wx_ssem, wx_rsem, a_ssem, a_rsem, b_ssem, b_rsem, self_sem, g_ssem, g_rsem, s_ssem, s_rsem,
+):
+    s = lax.axis_index("section")
+    q = lax.axis_index("seq")
+    x = lax.axis_index("expert")
+    l, c = s // 2, s % 2
+    yh, z = q // 8, q % 8
+    me = z * 2 + c
+
+    def dev(x_, l_, c_, yh_, z_):
+        return (l_ * 2 + c_, yh_ * 8 + z_, x_)
+
+    xr, xl, xo = (x + 1) % 4, (x + 3) % 4, (x + 2) % 4
+    right, left = dev(xr, l, c, yh, z), dev(xl, l, c, yh, z)
+    across, sibling = dev(x, 1 - l, c, yh, z), dev(x, l, 1 - c, yh, z)
+
+    def peer(wave, d):
+        if wave == 0:
+            return dev(x, l, d % 2, yh, d // 2)
+        return dev(x, 1 - l, d % 2, 1 - yh, d // 2)
+
+    w_local = [
+        pltpu.make_async_copy(w_in_hbm.at[c], win.at[pl.ds(0, FS)], w_sem.at[0]),
+        pltpu.make_async_copy(w_out_hbm.at[c], wout.at[pl.ds(0, FS)], w_sem.at[1]),
+    ]
+    for cp in w_local:
+        cp.start()
+
+    barrier = pltpu.get_barrier_semaphore()
+    for there in (right, left, across):
+        pl.semaphore_signal(barrier, inc=1, device_id=there, device_id_type=MESH)
+
+    @pl.loop(1, PEERS)
+    def _(i):
+        pl.semaphore_signal(barrier, inc=1, device_id=peer(0, (me + i) % PEERS), device_id_type=MESH)
+
+    @pl.loop(0, PEERS)
+    def _(i):
+        pl.semaphore_signal(barrier, inc=1, device_id=peer(1, (me + i) % PEERS), device_id_type=MESH)
+
+    ids_c, ids_r = ids_col_ref[...], ids_row_ref[...]
+    sub = lax.broadcasted_iota(jnp.int32, (TOK, TOK), 0)
+    lane = lax.broadcasted_iota(jnp.int32, (TOK, TOK), 1)
+    same = ids_c == ids_r
+    rank_c = jnp.sum(jnp.where(same & (lane < sub), 1.0, 0.0), axis=1, keepdims=True)
+    rank_r = jnp.sum(jnp.where(same & (sub < lane), 1.0, 0.0), axis=0, keepdims=True)
+
+    def slot(ids, rank):
+        hi = jnp.where(ids >= PEERS, 1, 0)
+        wave = hi + yh - 2 * hi * yh
+        return ((wave * PEERS + ids - hi * PEERS) * 3).astype(jnp.float32) + rank
+
+    perm = (slot(ids_r, rank_r) == sub.astype(jnp.float32)).astype(jnp.bfloat16)
+    perm_t = (slot(ids_c, rank_c) == lane.astype(jnp.float32)).astype(jnp.bfloat16)
+
+    def dot(a, b):
+        return jnp.dot(a, b, preferred_element_type=jnp.float32)
+
+    def pack(rows):
+        return dot(pack_ref[...], jnp.concatenate([rows[:, g * SEG : (g + 1) * SEG] for g in range(SEGS)], axis=0)).astype(jnp.bfloat16)
+
+    def a_copy(wave, d):
+        return pltpu.make_async_remote_copy(
+            src_ref=out_msg.at[wave, d], dst_ref=in_msg.at[wave, me],
+            send_sem=a_ssem.at[wave, d], recv_sem=a_rsem.at[wave, me],
+            device_id=peer(wave, d), device_id_type=MESH,
+        )
+
+    def a_recv(wave, d):
+        return pltpu.make_async_remote_copy(
+            src_ref=out_msg.at[wave, d], dst_ref=in_msg.at[wave, d],
+            send_sem=a_ssem.at[wave, d], recv_sem=a_rsem.at[wave, d],
+            device_id=peer(wave, d), device_id_type=MESH,
+        )
+
+    def b_copy(wave, d):
+        return pltpu.make_async_remote_copy(
+            src_ref=ret_msg.at[wave, d], dst_ref=ret_in.at[wave, me],
+            send_sem=b_ssem.at[wave, d], recv_sem=b_rsem.at[wave, me],
+            device_id=peer(wave, d), device_id_type=MESH,
+        )
+
+    def b_recv(wave, d):
+        return pltpu.make_async_remote_copy(
+            src_ref=ret_msg.at[wave, d], dst_ref=ret_in.at[wave, d],
+            send_sem=b_ssem.at[wave, d], recv_sem=b_rsem.at[wave, d],
+            device_id=peer(wave, d), device_id_type=MESH,
+        )
+
+    def each_peer(wave, act):
+        @pl.loop(1 if wave == 0 else 0, PEERS)
+        def _(i):
+            act((me + i) % PEERS)
+
+    self_a = pltpu.make_async_copy(out_msg.at[0, me], in_msg.at[0, me], self_sem.at[0])
+    self_b = pltpu.make_async_copy(ret_msg.at[0, me], ret_in.at[0, me], self_sem.at[1])
+
+    def outgoing(wave):
+        rows = dot(perm[wave * HALF : (wave + 1) * HALF], normed_ref[...]).astype(jnp.bfloat16)
+        out_msg[wave] = pack(rows).reshape(PEERS, MSG, SEG)
+
+    outgoing(0)
+    pl.semaphore_wait(barrier, 34)
+    each_peer(0, lambda d: a_copy(0, d).start())
+    self_a.start()
+    outgoing(1)
+    each_peer(1, lambda d: a_copy(1, d).start())
+
+    w_swap = [
+        pltpu.make_async_remote_copy(
+            src_ref=hbm.at[1 - c], dst_ref=vmem.at[pl.ds(FS, FS)], send_sem=wx_ssem.at[i], recv_sem=wx_rsem.at[i],
+            device_id=sibling, device_id_type=MESH,
+        )
+        for i, (hbm, vmem) in enumerate(((w_in_hbm, win), (w_out_hbm, wout)))
+    ]
+    for cp in w_swap:
+        cp.start()
+
+    own, mate = x * 2 + l, x * 2 + 1 - l
+
+    def blk(x_, far=False):
+        return x_ * 2 + (1 - l if far else l)
+
+    gather = [
+        (own, PP, across, mate),
+        (own, QQ, right, blk(xl)),
+        (own, QQ, left, blk(xr)),
+        (own, PP, right, blk(xl)),
+        (own, PP, left, blk(xr)),
+        (own, QQ, across, mate),
+        (mate, PP, right, blk(xl, True)),
+        (mate, PP, left, blk(xr, True)),
+        (blk(xl), QA, right, blk(xo)),
+        (blk(xr), QB, left, blk(xo)),
+        (blk(xl), QQ, across, blk(xl, True)),
+        (blk(xr), QQ, across, blk(xr, True)),
+        (blk(xl), PA, right, blk(xo)),
+        (blk(xr), PB, left, blk(xo)),
+        (blk(xl, True), PA, right, blk(xo, True)),
+        (blk(xr, True), PB, left, blk(xo, True)),
+        (blk(xo), QA, across, blk(xo, True)),
+        (blk(xo), QB, across, blk(xo, True)),
+    ]
+
+    def g_copy(wave, i, received=False):
+        sent, cols, there, got = gather[i]
+        ref = xg.at[wave, got if received else sent, :, pl.ds(*cols)]
+        return pltpu.make_async_remote_copy(
+            src_ref=ref, dst_ref=ref, send_sem=g_ssem.at[wave, i], recv_sem=g_rsem.at[wave, i],
+            device_id=there, device_id_type=MESH,
+        )
+
+    def g_start(wave, *which):
+        for i in which:
+            g_copy(wave, i).start()
+
+    def g_wait(wave, *which):
+        for i in which:
+            g_copy(wave, i, True).wait_recv()
+
+    def arrive(wave):
+        if wave == 0:
+            self_a.wait()
+        each_peer(wave, lambda d: a_recv(wave, d).wait_recv())
+        rows = dot(unpack_ref[...], in_msg[wave].reshape(PEERS * MSG, SEG)).astype(jnp.bfloat16)
+        for g in range(SEGS):
+            xg[wave, own, :, pl.ds(g * SEG, SEG)] = rows[g * HALF : (g + 1) * HALF]
+
+    def gather_1(wave):
+        g_start(wave, 0, 1, 2, 3, 4, 5)
+
+    def gather_2(wave):
+        g_wait(wave, 0)
+        g_start(wave, 6, 7)
+        g_wait(wave, 1, 2)
+        g_start(wave, 8, 9, 10, 11)
+
+    def gather_3(wave):
+        g_wait(wave, 3, 4)
+        g_start(wave, 12, 13)
+        g_wait(wave, 6, 7)
+        g_start(wave, 14, 15)
+        g_wait(wave, 8, 9)
+        g_start(wave, 16, 17)
+
+    def gather_4(wave):
+        g_wait(wave, 5, 10, 11, 12, 13, 14, 15, 16, 17)
+
+    def hidden(wave):
+        rows = xg[wave].reshape(8 * HALF, D)
+        units = lax.dot_general(rows, win[...], (((1,), (1,)), ((), ())), preferred_element_type=jnp.float32)
+        hid[...] = jnp.maximum(units, 0.0).astype(jnp.bfloat16)
+
+    def partial(wave, cols):
+        part = dot(hid[...], wout[:, pl.ds(*cols)])
+        pt[wave, :, :, pl.ds(*cols)] = part.astype(jnp.bfloat16).reshape(8, HALF, cols[1])
+
+    def span(home, cols):
+        return lambda wave: pt.at[wave, home, :, pl.ds(*cols)]
+
+    def inner(buf, i, cols):
+        return lambda wave: buf.at[wave, i, :, pl.ds(*cols)]
+
+    sums = []
+    for f in (1, 0):
+        far = f == 1
+        sums += [
+            (span(blk(xo, far), PA), inner(r_p2r, f, PA), left),
+            (span(blk(xo, far), PB), inner(r_p2l, f, PA), right),
+            (span(blk(xl, far), PB), inner(r_pr, f, PB), left),
+            (span(blk(xr, far), PA), inner(r_pl, f, PA), right),
+            (span(blk(xl, far), PA), inner(r_pr, f, PA), left),
+            (span(blk(xr, far), PB), inner(r_pl, f, PB), right),
+        ]
+    q0, q1 = (0, QA[1]), (QA[1], QB[1])
+    sums += [
+        (span(mate, PP), inner(r_py, 0, PP), across),
+        (span(blk(xo, True), QQ), inner(r_qy, 0, (0, QQ[1])), across),
+        (span(blk(xl, True), QQ), inner(r_qy, 1, (0, QQ[1])), across),
+        (span(blk(xr, True), QQ), inner(r_qy, 2, (0, QQ[1])), across),
+        (span(mate, QQ), inner(r_qy, 3, (0, QQ[1])), across),
+        (span(blk(xo), QA), inner(r_q2r, 0, q0), left),
+        (span(blk(xo), QB), inner(r_q2l, 0, q0), right),
+        (span(blk(xl), QB), inner(r_qr, 0, q1), left),
+        (span(blk(xr), QA), inner(r_ql, 0, q0), right),
+        (span(blk(xl), QA), inner(r_qr, 0, q0), left),
+        (span(blk(xr), QB), inner(r_ql, 0, q1), right),
+    ]
+
+    def s_copy(wave, i):
+        src, dst, there = sums[i]
+        return pltpu.make_async_remote_copy(
+            src_ref=src(wave), dst_ref=dst(wave), send_sem=s_ssem.at[wave, i], recv_sem=s_rsem.at[wave, i],
+            device_id=there, device_id_type=MESH,
+        )
+
+    def s_start(wave, *which):
+        for i in which:
+            s_copy(wave, i).start()
+
+    def s_wait(wave, *which):
+        for i in which:
+            s_copy(wave, i).wait_recv()
+
+    def add(wave, home, cols, *terms):
+        step = 128
+
+        @pl.loop(0, cols[1] // step)
+        def _(i):
+            here = pl.ds(pl.multiple_of(cols[0] + i * step, 128), step)
+            total = pt[wave, home, :, here].astype(jnp.float32)
+            for buf, j, first in terms:
+                total += buf[wave, j, :, pl.ds(pl.multiple_of(first + i * step, 128), step)].astype(jnp.float32)
+            pt[wave, home, :, here] = total.astype(jnp.bfloat16)
+
+    def sum_p2(wave):
+        for n, f in ((0, 1), (6, 0)):
+            far = f == 1
+            s_wait(wave, n, n + 1)
+            add(wave, blk(xl, far), PA, (r_p2r, f, 0))
+            s_start(wave, n + 4)
+            add(wave, blk(xr, far), PB, (r_p2l, f, 0))
+            s_start(wave, n + 5)
+
+    def sum_p1(wave):
+        for n, f in ((0, 1), (6, 0)):
+            s_wait(wave, n + 2, n + 3, n + 4, n + 5)
+            add(wave, blk(x, f == 1), PP, (r_pr, f, 0), (r_pl, f, 0))
+            if f == 1:
+                s_start(wave, 12)
+
+    def sum_py(wave):
+        s_wait(wave, 12)
+        add(wave, own, PP, (r_py, 0, 0))
+
+    def sum_qy(wave):
+        s_wait(wave, 13)
+        add(wave, blk(xo), QQ, (r_qy, 0, 0))
+        s_start(wave, 17, 18)
+        s_wait(wave, 14)
+        add(wave, blk(xl), QQ, (r_qy, 1, 0))
+        s_start(wave, 19)
+        s_wait(wave, 15)
+        add(wave, blk(xr), QQ, (r_qy, 2, 0))
+        s_start(wave, 20)
+
+    def sum_q2(wave):
+        s_wait(wave, 17, 18)
+        add(wave, blk(xl), QA, (r_q2r, 0, 0))
+        s_start(wave, 21)
+        add(wave, blk(xr), QB, (r_q2l, 0, 0))
+        s_start(wave, 22)
+
+    def sum_q1(wave):
+        s_wait(wave, 16, 19, 20, 21, 22)
+        add(wave, own, QQ, (r_qy, 3, 0), (r_qr, 0, 0), (r_ql, 0, 0))
+
+    def send_back(wave):
+        ret_msg[wave] = pack(pt[wave, own]).reshape(PEERS, MSG, SEG)
+        each_peer(wave, lambda d: b_copy(wave, d).start())
+        if wave == 0:
+            self_b.start()
+
+    def come_back(wave):
+        if wave == 0:
+            self_b.wait()
+        each_peer(wave, lambda d: b_recv(wave, d).wait_recv())
+        fin[wave] = dot(unpack_ref[...], ret_in[wave].reshape(PEERS * MSG, SEG)).astype(jnp.bfloat16)
+
+    def partials(wave):
+        partial(wave, PA)
+        s_start(wave, 0, 6, 3, 9)
+        partial(wave, QA)
+        partial(wave, QB)
+        s_start(wave, 13, 14, 15, 16)
+        partial(wave, PB)
+        s_start(wave, 1, 7, 2, 8)
+
+    arrive(0)
+    gather_1(0)
+    gather_2(0)
+    arrive(1)
+    gather_3(0)
+    gather_1(1)
+    gather_4(0)
+    for cp in w_local:
+        cp.wait()
+    for cp in w_swap:
+        cp.wait_recv()
+    hidden(0)
+    gather_2(1)
+    partials(0)
+    gather_3(1)
+    sum_qy(0)
+    sum_p2(0)
+    gather_4(1)
+    hidden(1)
+    sum_q2(0)
+    sum_p1(0)
+    partials(1)
+    sum_q1(0)
+    sum_py(0)
+    send_back(0)
+    sum_qy(1)
+    sum_p2(1)
+    sum_q2(1)
+    sum_p1(1)
+    sum_q1(1)
+    sum_py(1)
+    send_back(1)
+    come_back(0)
+    come_back(1)
+
+    for g in range(SEGS):
+        cols = pl.ds(g * SEG, SEG)
+        rows = jnp.concatenate([fin[0, pl.ds(g * HALF, HALF)], fin[1, pl.ds(g * HALF, HALF)]], axis=0)
+        expert_out = dot(perm_t, rows)
+        out_ref[:, cols] = (state_ref[:, cols] + scale_ref[...] * expert_out).astype(jnp.bfloat16)
+
+    for cp in w_swap:
+        cp.wait_send()
+    for wave in (0, 1):
+        each_peer(wave, lambda d: a_recv(wave, d).wait_send())
+        each_peer(wave, lambda d: b_recv(wave, d).wait_send())
+        for i in range(len(gather)):
+            g_copy(wave, i).wait_send()
+        for i in range(len(sums)):
+            s_copy(wave, i).wait_send()
+
+
+def expert_layer(normed, state, ids, scale, w_in, w_out):
+    order = message_order()
+    vmem = pl.BlockSpec(memory_space=pltpu.VMEM)
+    hbm = pl.BlockSpec(memory_space=pl.ANY)
+    bf = jnp.bfloat16
+    return pl.pallas_call(
+        moe_kernel,
+        out_shape=jax.ShapeDtypeStruct((TOK, D), bf),
+        in_specs=[vmem] * 7 + [hbm] * 2,
+        out_specs=vmem,
+        scratch_shapes=[
+            pltpu.VMEM((2 * FS, D), bf),
+            pltpu.VMEM((2 * FS, D), bf),
+            pltpu.VMEM((8 * HALF, 2 * FS), bf),
+            pltpu.VMEM((2, 8, HALF, D), bf),
+            pltpu.VMEM((2, 8, HALF, D), bf),
+            pltpu.VMEM((2, PEERS, MSG, SEG), bf),
+            pltpu.VMEM((2, PEERS, MSG, SEG), bf),
+            pltpu.VMEM((2, PEERS, MSG, SEG), bf),
+            pltpu.VMEM((2, PEERS, MSG, SEG), bf),
+            pltpu.VMEM((2, PEERS * MSG, SEG), bf),
+            pltpu.VMEM((2, 2, HALF, PA[1]), bf),
+            pltpu.VMEM((2, 2, HALF, PB[1]), bf),
+            pltpu.VMEM((2, 2, HALF, PP[1]), bf),
+            pltpu.VMEM((2, 2, HALF, PP[1]), bf),
+            pltpu.VMEM((2, 1, HALF, PP[1]), bf),
+            pltpu.VMEM((2, 4, HALF, QQ[1]), bf),
+            pltpu.VMEM((2, 1, HALF, QA[1]), bf),
+            pltpu.VMEM((2, 1, HALF, QB[1]), bf),
+            pltpu.VMEM((2, 1, HALF, QQ[1]), bf),
+            pltpu.VMEM((2, 1, HALF, QQ[1]), bf),
+            pltpu.SemaphoreType.DMA((2,)),
+            pltpu.SemaphoreType.DMA((2,)),
+            pltpu.SemaphoreType.DMA((2,)),
+            pltpu.SemaphoreType.DMA((2, PEERS)),
+            pltpu.SemaphoreType.DMA((2, PEERS)),
+            pltpu.SemaphoreType.DMA((2, PEERS)),
+            pltpu.SemaphoreType.DMA((2, PEERS)),
+            pltpu.SemaphoreType.DMA((2,)),
+            pltpu.SemaphoreType.DMA((2, 18)),
+            pltpu.SemaphoreType.DMA((2, 18)),
+            pltpu.SemaphoreType.DMA((2, 23)),
+            pltpu.SemaphoreType.DMA((2, 23)),
+        ],
+        compiler_params=pltpu.CompilerParams(
+            collective_id=0, has_side_effects=True, vmem_limit_bytes=60 * 2**20
+        ),
+    )(
+        jnp.asarray(order, bf),
+        jnp.asarray(order.T, bf),
+        normed,
+        state,
+        ids.reshape(TOK, 1),
+        ids.reshape(1, TOK),
+        scale.reshape(TOK, 1),
+        w_in,
+        w_out,
+    )
+
+
 def body(
     queries, dec_state, enc_kv, band_start, norm_gain, route_ids, keep, route_prob, w_in, w_out
 ):
@@ -68,41 +530,8 @@
     normed = (
         state * lax.rsqrt(jnp.mean(state * state, axis=-1, keepdims=True) + 1e-06) * norm_gain
     ).astype(jnp.bfloat16)
-    experts_of = route_ids[0, :, 0]
-    tok_count = experts_of.shape[0]
-    seq_count = lax.axis_size("seq")
-    per_device = w_in.shape[0]
-    expert_count = per_device * seq_count
-    capacity = max(2, tok_count // expert_count)
-    one_hot = (experts_of[:, None] == jnp.arange(expert_count, dtype=jnp.int32)[None, :]).astype(
-        jnp.int32
-    )
-    earlier = jnp.cumsum(one_hot, axis=0) - one_hot
-    slot_of = jnp.sum(earlier * one_hot, axis=1)
-    target = experts_of * capacity + slot_of
-    kept = keep[0] == 1
-    slot_ids = jnp.arange(expert_count * capacity, dtype=jnp.int32)
-    dispatch = ((slot_ids[:, None] == target[None, :]) & kept[None, :]).astype(jnp.bfloat16)
-    outgoing = jnp.dot(dispatch, normed, preferred_element_type=jnp.float32).astype(jnp.bfloat16)
-    outgoing = outgoing.reshape(seq_count, per_device, capacity, D)
-    arrived = lax.all_to_all(outgoing, "seq", split_axis=0, concat_axis=2, tiled=True)[0]
-    hidden = jnp.einsum(
-        "emd,efd->emf",
-        lax.all_gather(arrived, ("section", "expert"), axis=1, tiled=True),
-        w_in,
-        preferred_element_type=jnp.float32,
-    )
-    hidden = jnp.maximum(hidden, 0.0).astype(jnp.bfloat16)
-    partials = jnp.einsum("emf,efd->emd", hidden, w_out, preferred_element_type=jnp.float32)
-    summed = lax.psum_scatter(
-        partials.astype(jnp.bfloat16), ("section", "expert"), scatter_dimension=1, tiled=True
-    )
-    returned = lax.all_to_all(summed, "seq", split_axis=1, concat_axis=0, tiled=True).reshape(
-        expert_count * capacity, D
-    )
-    expert_out = jnp.einsum("st,sd->td", dispatch, returned, preferred_element_type=jnp.float32)
-    scale = (keep[0].astype(jnp.float32) * route_prob[0])[:, None]
-    return (state + scale * expert_out).astype(jnp.bfloat16)[None]
+    scale = keep[0].astype(jnp.float32) * route_prob[0]
+    return expert_layer(normed, state, route_ids[0], scale, w_in, w_out)[None]
 
 
 def solution(mesh):

time: 386 us -> 176 us (0.46)
  waiting for transfers between devices: 257 us -> 15.2 us
  Pallas kernels: 0 us -> 132 us
  matrix products: 41 us -> 3.03 us
  blocking collectives: 27.7 us -> 0 us
  between operations: 14.2 us -> 0.78 us
  starting transfers between devices: 17.8 us -> 7.55 us
  local copies, waits for them, and re-layouts: 23 us -> 13 us
    reduce_scatter x1 -> x0, waiting for transfers between devices: 143 us -> none  [body(): lax.psum_scatter(partials.astype(jnp.bfloat16), ('section', 'expert'), sc...]
    pallas_call x0 -> x1, Pallas kernels: none -> 132 us  [expert_layer(): pl.pallas_call(moe_kernel, out_shape=jax.ShapeDtypeStruct((TOK, D), bf),...]
    all_gather x1 -> x0, waiting for transfers between devices: 78.8 us -> none  [body(): lax.all_gather(arrived, ('section', 'expert'), axis=1, tiled=True)]
    dot_general x4 -> x0, matrix products: 38 us -> none  [the longest x1 22 us: body(): jnp.einsum('emd,efd->emf', lax.all_gather(arrived, ('section', 'expert'),...]
    all_to_all x1 -> x0, blocking collectives: 27.7 us -> none  [body(): lax.all_to_all(outgoing, 'seq', split_axis=0, concat_axis=2, tiled=True)[0]]
    all_to_all x1 -> x0, waiting for transfers between devices: 21 us -> none  [body(): lax.all_to_all(summed, 'seq', split_axis=1, concat_axis=0, tiled=True)]
    all_to_all x1 -> x0, starting transfers between devices: 9.26 us -> none  [body(): lax.all_to_all(summed, 'seq', split_axis=1, concat_axis=0, tiled=True)]
    reshape x3 -> x0, local copies, waits for them, and re-layouts: 3.89 us -> none  [the longest x2 2.44 us: body(): outgoing = outgoing.reshape(seq_count, per_device, capacity, D)]
  transfers between devices with their start and end apart: 6 -> 3, of which waited for: 6 -> 3; matrix products, arithmetic and copies ran while one was open for 2% -> 4% of each run, Pallas kernels for 0% -> 0%
where the time goes in v1:
time: 176 us
  Pallas kernels  132 us (75%)
  waiting for transfers between devices  15.2 us (9%)
  local copies, waits for them, and re-layouts  13 us (7%)
  starting transfers between devices  7.55 us (4%)
  other arithmetic  4.91 us (3%)
  matrix products  3.03 us (2%)
    pallas_call x1, Pallas kernels, expert_layer(): pl.pallas_call(moe_kernel, out_shape=jax.ShapeDtypeStruct((TOK, D), bf),...  132 us
    ppermute x1, waiting for transfers between devices, shifted(): return lax.ppermute(block, axis, route)  7.85 us
    ppermute x1, waiting for transfers between devices, extended(): lax.ppermute(head, axis, [((i + 1) % count, i) for i in range(ends)])  3.77 us
    ppermute x1, starting transfers between devices, extended(): lax.ppermute(tail, axis, [(i, (i + 1) % count) for i in range(ends)])  3.57 us
    ppermute x1, waiting for transfers between devices, extended(): lax.ppermute(tail, axis, [(i, (i + 1) % count) for i in range(ends)])  3.54 us
  transfers between devices with their start and end apart: 3, of which 3 were waited for; matrix products, arithmetic and copies ran while one was open for 4% of the time, Pallas kernels for 0%

profile of v1, /device:TPU:1, one launch (start us, length us, event | category | flops | bytes accessed | tf_op | source)
XLA Modules:
  0.0 176.1 jit_solution(2867315028375918534)
XLA Ops:
  0.0 0.0 copy-start
  0.0 2.7 %collective-permute-start = (bf16[2,160,1024]{2,1,0:T(8,128)(2,1)}, bf16[2,160,1024]{2,1,0:T(8,128)(2,1)S(1)}, u32[]{:S(2)}, u32[]{:S(2)}) collective-permute-start(bf16[2,160,1024]{2,1,0:T(8,128)(2,1)} %bitcast.44), channel_id=1, source_target_pairs={{192,0},{0,64},{64,128},{128,192},{193,1},{1,65},{65,129},{129,193... | collective-permute-start | bytes 1966088 | tf_op jit(solution)/shard_map/ppermute | solution.py:36
  2.7 7.8 %collective-permute-done = bf16[2,160,1024]{2,1,0:T(8,128)(2,1)S(1)} collective-permute-done((bf16[2,160,1024]{2,1,0:T(8,128)(2,1)}, bf16[2,160,1024]{2,1,0:T(8,128)(2,1)S(1)}, u32[]{:S(2)}, u32[]{:S(2)}) %collective-permute-start) | collective-permute-done | bytes 655392 | tf_op jit(solution)/shard_map/ppermute | solution.py:36
  10.5 3.6 %collective-permute-start.1 = (bf16[2,160,1024]{2,1,0:T(8,128)(2,1)S(1)}, bf16[2,160,1024]{2,1,0:T(8,128)(2,1)S(1)}, u32[]{:S(2)}, u32[]{:S(2)}) collective-permute-start(bf16[2,160,1024]{2,1,0:T(8,128)(2,1)S(1)} %collective-permute-done), channel_id=1, source_target_pairs={{0,4},{4,8},{8,12},{12,16},{16,20},{20,24},{24,28},{28,32},{32,36}... | collective-permute-start | bytes 1966088 | tf_op jit(solution)/shard_map/ppermute | solution.py:47
  14.1 1.3 collective-permute-start.2
  16.1 3.0 %reshape_squeeze.14 = bf16[96,8,4,128]{3,2,1,0:T(4,128)(2,1)} reshape(bf16[1,96,4096]{2,1,0:T(8,128)(2,1)} %param.12) | data formatting | bytes 1572864 | tf_op jit(solution)/shard_map/reshape;squeeze | solution.py:59
  19.1 0.0 copy-done
  19.1 0.0 copy-start.5
  19.1 0.0 copy-start.6
  19.1 0.0 copy-start.4
  19.1 2.3 %reshape.44 = f32[96,8,4,128]{3,2,1,0:T(4,128)} reshape(bf16[1,96,4096]{2,1,0:T(8,128)(2,1)S(1)} %copy-done) | data formatting | bytes 2359296 | tf_op jit(solution)/shard_map/convert_element_type | solution.py:529
  21.4 0.0 copy-done.5
  21.4 0.0 copy-done.6
  21.4 0.7 copy.35.scale_ref
  22.1 0.0 copy-done.4
  22.1 0.7 copy.34.ids_col_ref
  22.8 0.5 copy.27
  23.3 3.5 %collective-permute-done.1 = bf16[2,160,1024]{2,1,0:T(8,128)(2,1)S(1)} collective-permute-done((bf16[2,160,1024]{2,1,0:T(8,128)(2,1)S(1)}, bf16[2,160,1024]{2,1,0:T(8,128)(2,1)S(1)}, u32[]{:S(2)}, u32[]{:S(2)}) %collective-permute-start.1) | collective-permute-done | bytes 655392 | tf_op jit(solution)/shard_map/ppermute | solution.py:47
  26.9 0.5 copy.26
  27.4 3.8 %collective-permute-done.2 = bf16[2,160,1024]{2,1,0:T(8,128)(2,1)} collective-permute-done((bf16[2,160,1024]{2,1,0:T(8,128)(2,1)S(1)}, bf16[2,160,1024]{2,1,0:T(8,128)(2,1)}, u32[]{:S(2)}, u32[]{:S(2)}) %collective-permute-start.2) | collective-permute-done | bytes 655392 | tf_op jit(solution)/shard_map/ppermute | solution.py:49
  31.2 1.4 copy.28
  32.6 0.0 copy-start.1
  32.6 1.0 fusion.9
  33.6 0.1 copy-done.1
  33.7 0.0 copy-start.2
  33.7 0.8 bitcast_reduce_fusion
  34.5 1.1 fusion.3
  35.6 0.0 copy-done.2
  35.6 2.2 %fusion.2 = (f32[96]{0:T(128)S(1)}, f32[96,8,4,128]{3,0,2,1:T(8,128)S(1)}) fusion(f32[96,8,4,128]{3,2,1,0:T(4,128)S(1)} %copy-done.2, f32[96,8,4]{0,2,1:T(4,128)S(1)} %bitcast.41, bf16[128,8,128,1]{0,2,3,1:T(8,128)(2,1)S(1)} %bitcast.40, f32[8,128,96,4]{1,2,3,0:T(8,128)S(1)} %get-tuple-element.10, f32[8,4,96]{2,1,0:T(4,128)S(1)} %get-tuple-element.9), kind=kOutput, calls=%fused_computation.10 | convolution fusion | flops 103022496 | bytes 5005696 | tf_op jit(solution)/shard_map/kgtw,wkd->tkgd/dot_general | solution.py:69
  37.8 1.0 copy.32
  38.9 0.0 copy-start.3
  38.9 0.6 reshape.42
  39.5 0.1 copy-done.3
  39.6 2.8 %multiply_convert_fusion = (bf16[96,4096]{1,0:T(8,128)(2,1)}, f32[96,4096]{1,0:T(8,128)}) fusion(f32[4096]{0:T(1024)S(1)} %copy-done.3, f32[96]{0:T(128)S(1)} %add_rsqrt_fusion, f32[96,4096]{1,0:T(8,128)S(1)} %reshape.42, bf16[1,96,4096]{2,1,0:T(8,128)(2,1)} %param.13), kind=kLoop, calls=%fused_computation.11 | loop fusion | flops 1966080 | bytes 4735360 | tf_op jit(solution)/shard_map/convert_element_type | solution.py:532
  42.4 131.6 %shard_map.118 = bf16[96,4096]{1,0:T(8,128)(2,1)} custom-call(bf16[384,384]{1,0:T(8,128)(2,1)} %constant.31.clone.unpack_ref, bf16[384,384]{1,0:T(8,128)(2,1)} %constant.32.clone.pack_ref, bf16[96,4096]{1,0:T(8,128)(2,1)} %get-tuple-element.5.normed_ref, f32[96,4096]{1,0:T(8,128)} %get-tuple-element.6.state_ref, s32[96,1]{1,0:T(8,128)} %copy.34.ids_col_ref, ...), custom_call_target="tpu_custom_call" | custom-call | tf_op jit(solution)/shard_map/pallas_call | solution.py:463
  174.0 2.1 %copy.53 = bf16[1,96,4096]{2,1,0:T(8,128)(2,1)} copy(bf16[1,96,4096]{2,1,0:T(8,128)(2,1)} %bitcast.38) | data formatting | bytes 1572864
  (3 shorter events, 0.0 us)
Async XLA Ops:
  0.0 19.1 %copy-start = (bf16[1,96,4096]{2,1,0:T(8,128)(2,1)S(1)}, bf16[1,96,4096]{2,1,0:T(8,128)(2,1)}, u32[]{:S(2)}) copy-start(bf16[1,96,4096]{2,1,0:T(8,128)(2,1)} %param.13) | copy-start | bytes 2359300
  0.0 10.5 %collective-permute-start = (bf16[2,160,1024]{2,1,0:T(8,128)(2,1)}, bf16[2,160,1024]{2,1,0:T(8,128)(2,1)S(1)}, u32[]{:S(2)}, u32[]{:S(2)}) collective-permute-start(bf16[2,160,1024]{2,1,0:T(8,128)(2,1)} %bitcast.44), channel_id=1, source_target_pairs={{192,0},{0,64},{64,128},{128,192},{193,1},{1,65},{65,129},{129,193... | collective-permute-start | bytes 1966088 | tf_op jit(solution)/shard_map/ppermute | solution.py:36
  10.5 16.3 %collective-permute-start.1 = (bf16[2,160,1024]{2,1,0:T(8,128)(2,1)S(1)}, bf16[2,160,1024]{2,1,0:T(8,128)(2,1)S(1)}, u32[]{:S(2)}, u32[]{:S(2)}) collective-permute-start(bf16[2,160,1024]{2,1,0:T(8,128)(2,1)S(1)} %collective-permute-done), channel_id=1, source_target_pairs={{0,4},{4,8},{8,12},{12,16},{16,20},{20,24},{24,28},{28,32},{32,36}... | collective-permute-start | bytes 1966088 | tf_op jit(solution)/shard_map/ppermute | solution.py:47
  14.1 17.0 %collective-permute-start.2 = (bf16[2,160,1024]{2,1,0:T(8,128)(2,1)S(1)}, bf16[2,160,1024]{2,1,0:T(8,128)(2,1)}, u32[]{:S(2)}, u32[]{:S(2)}) collective-permute-start(bf16[2,160,1024]{2,1,0:T(8,128)(2,1)S(1)} %collective-permute-done), channel_id=1, source_target_pairs={{4,0},{8,4},{12,8},{16,12},{20,16},{24,20},{28,24},{32,28},{36,32}... | collective-permute-start | bytes 1966088 | tf_op jit(solution)/shard_map/ppermute | solution.py:49
  19.1 2.3 %copy-start.5 = (f32[1,96]{1,0:T(1,128)S(1)}, f32[1,96]{1,0:T(1,128)}, u32[]{:S(2)}) copy-start(f32[1,96]{1,0:T(1,128)} %param.19) | copy-start | bytes 1156
  19.1 2.3 %copy-start.6 = (s32[1,96]{1,0:T(1,128)S(1)}, s32[1,96]{1,0:T(1,128)}, u32[]{:S(2)}) copy-start(s32[1,96]{1,0:T(1,128)} %param.18) | copy-start | bytes 1156
  19.1 3.1 %copy-start.4 = (s32[1,96,1]{1,2,0:T(1,128)S(1)}, s32[1,96,1]{1,2,0:T(1,128)}, u32[]{:S(2)}) copy-start(s32[1,96,1]{1,2,0:T(1,128)} %param.17) | copy-start | bytes 1156
  32.6 1.1 copy-start.1
  33.7 1.9 %copy-start.2 = (f32[96,8,4,128]{3,2,1,0:T(4,128)S(1)}, f32[96,8,4,128]{3,2,1,0:T(4,128)}, u32[]{:S(2)}) copy-start(f32[96,8,4,128]{3,2,1,0:T(4,128)} %reshape.44) | copy-start | bytes 4718596
  38.9 0.7 copy-start.3

commit v2 on v1

--- a/solution.py
+++ b/solution.py
@@ -28,47 +28,9 @@
 QB = (3200, 896)
 PP = (0, 2304)
 QQ = (2304, 1792)
-
-
-def shifted(block, axis, distance):
-    devices = range(lax.axis_size(axis))
-    route = [((i - distance) % len(devices), i) for i in devices]
-    return lax.ppermute(block, axis, route)
-
-
-def extended(cells, sides, width):
-    for axis, dim in sides:
-        count = lax.axis_size(axis)
-        ends = count - 1
-        head = lax.slice_in_dim(cells, 0, width, axis=dim)
-        tail = lax.slice_in_dim(cells, cells.shape[dim] - width, cells.shape[dim], axis=dim)
-        cells = jnp.concatenate(
-            [
-                lax.ppermute(tail, axis, [(i, (i + 1) % count) for i in range(ends)]),
-                cells,
-                lax.ppermute(head, axis, [((i + 1) % count, i) for i in range(ends)]),
-            ],
-            axis=dim,
-        )
-    return cells
-
-
-def cross_attend(query_rows, band_pair):
-    tok_count = query_rows.shape[0]
-    groups = HEADS // KV_HEADS
-    grouped = query_rows.reshape(tok_count, KV_HEADS, groups, DH)
-    keys_b = band_pair[0].reshape(WIN, KV_HEADS, DH)
-    values_b = band_pair[1].reshape(WIN, KV_HEADS, DH)
-    scores = jnp.einsum(
-        "tkgd,wkd->kgtw", grouped, keys_b, preferred_element_type=jnp.float32
-    ) / math.sqrt(DH)
-    row_peak = jnp.max(scores, axis=-1, keepdims=True)
-    weights = jnp.exp(scores - row_peak)
-    row_total = jnp.sum(weights, axis=-1)
-    rounded = weights.astype(jnp.bfloat16)
-    context = jnp.einsum("kgtw,wkd->tkgd", rounded, values_b, preferred_element_type=jnp.float32)
-    context = context / jnp.transpose(row_total, (2, 0, 1))[..., None]
-    return context.reshape(tok_count, HEADS * DH)
+FR = 160
+KVC = 512
+GROUP = HEADS // KV_HEADS
 
 
 def message_order():
@@ -81,8 +43,11 @@
 
 
 def moe_kernel(
-    unpack_ref, pack_ref, normed_ref, state_ref, ids_col_ref, ids_row_ref, scale_ref, w_in_hbm, w_out_hbm,
+    first_ref, ids_ref, keep_ref, prob_ref, gain_ref,
+    unpack_hbm, pack_hbm, queries_hbm, dec_hbm, kv_hbm, w_in_hbm, w_out_hbm,
     out_ref,
+    unpack_ref, pack_ref, queries_ref, dec_ref, state_ref, normed_ref, kv,
+    in_sem, k_ssem, k_rsem, f_ssem, f_rsem, x_ssem,
     win, wout, hid, xg, pt, out_msg, in_msg, ret_msg, ret_in, fin,
     r_p2r, r_p2l, r_pr, r_pl, r_py, r_qy, r_q2r, r_q2l, r_qr, r_ql,
     w_sem, wx_ssem, wx_rsem, a_ssem, a_rsem, b_ssem, b_rsem, self_sem, g_ssem, g_rsem, s_ssem, s_rsem,
@@ -110,11 +75,23 @@
         pltpu.make_async_copy(w_in_hbm.at[c], win.at[pl.ds(0, FS)], w_sem.at[0]),
         pltpu.make_async_copy(w_out_hbm.at[c], wout.at[pl.ds(0, FS)], w_sem.at[1]),
     ]
-    for cp in w_local:
-        cp.start()
+    inputs = [
+        pltpu.make_async_copy(src, dst, in_sem.at[i])
+        for i, (src, dst) in enumerate(
+            (
+                (queries_hbm.at[0], queries_ref),
+                (dec_hbm.at[0], dec_ref),
+                (pack_hbm, pack_ref),
+                (unpack_hbm, unpack_ref),
+            )
+        )
+    ]
 
     barrier = pltpu.get_barrier_semaphore()
-    for there in (right, left, across):
+    corner = dev(x, 1 - l, 1 - c, yh, z)
+    after, before = ((s, (q + 1) % 16, x), (s, (q + 15) % 16, x))
+    opposite = dev(x, l, c, 1 - yh, z)
+    for there in (corner, opposite, after, before, right, left, across):
         pl.semaphore_signal(barrier, inc=1, device_id=there, device_id_type=MESH)
 
     @pl.loop(1, PEERS)
@@ -125,17 +102,29 @@
     def _(i):
         pl.semaphore_signal(barrier, inc=1, device_id=peer(1, (me + i) % PEERS), device_id_type=MESH)
 
-    ids_c, ids_r = ids_col_ref[...], ids_row_ref[...]
+    for cp in inputs:
+        cp.start()
+    for cp in w_local:
+        cp.start()
+
     sub = lax.broadcasted_iota(jnp.int32, (TOK, TOK), 0)
     lane = lax.broadcasted_iota(jnp.int32, (TOK, TOK), 1)
+
+    def column(row):
+        return jnp.sum(jnp.where(sub == lane, row, 0.0), axis=1, keepdims=True)
+
+    ids_r = ids_ref[...].astype(jnp.float32)
+    ids_c = column(ids_r)
+    scale = column(keep_ref[...].astype(jnp.float32) * prob_ref[...])
     same = ids_c == ids_r
     rank_c = jnp.sum(jnp.where(same & (lane < sub), 1.0, 0.0), axis=1, keepdims=True)
     rank_r = jnp.sum(jnp.where(same & (sub < lane), 1.0, 0.0), axis=0, keepdims=True)
 
     def slot(ids, rank):
-        hi = jnp.where(ids >= PEERS, 1, 0)
-        wave = hi + yh - 2 * hi * yh
-        return ((wave * PEERS + ids - hi * PEERS) * 3).astype(jnp.float32) + rank
+        hi = jnp.where(ids >= PEERS, 1.0, 0.0)
+        here = yh.astype(jnp.float32)
+        wave = hi + here - 2.0 * hi * here
+        return (wave * PEERS + ids - hi * PEERS) * 3.0 + rank
 
     perm = (slot(ids_r, rank_r) == sub.astype(jnp.float32)).astype(jnp.bfloat16)
     perm_t = (slot(ids_c, rank_c) == lane.astype(jnp.float32)).astype(jnp.bfloat16)
@@ -186,12 +175,72 @@
         rows = dot(perm[wave * HALF : (wave + 1) * HALF], normed_ref[...]).astype(jnp.bfloat16)
         out_msg[wave] = pack(rows).reshape(PEERS, MSG, SEG)
 
-    outgoing(0)
-    pl.semaphore_wait(barrier, 34)
-    each_peer(0, lambda d: a_copy(0, d).start())
-    self_a.start()
-    outgoing(1)
-    each_peer(1, lambda d: a_copy(1, d).start())
+    nxt = ((s + 1) % 4, q, x)
+
+    def chunk(i):
+        return i % 2, pl.ds((i // 2) * KVC, KVC)
+
+    def k_copy(i):
+        which, cols = chunk(i)
+        return pltpu.make_async_remote_copy(
+            src_ref=kv_hbm.at[which, 0, :, cols], dst_ref=kv.at[which, 1, :, cols],
+            send_sem=k_ssem.at[i], recv_sem=k_rsem.at[i], device_id=nxt, device_id_type=MESH,
+        )
+
+    RELAYED = 2
+    ring_after, ring_before = dev(x, l, c, yh, (z + 1) % 8), dev(x, l, c, yh, (z + 7) % 8)
+
+    def f_copy(i, up):
+        which, cols = chunk(i)
+        to = 0 if up else 2
+        if i < RELAYED:
+            there = ring_after if up else ring_before
+        else:
+            there = after if up else before
+        return pltpu.make_async_remote_copy(
+            src_ref=kv.at[which, 1, :, cols], dst_ref=kv.at[which, to, :, cols],
+            send_sem=f_ssem.at[i, to // 2], recv_sem=f_rsem.at[i, to // 2],
+            device_id=there, device_id_type=MESH,
+        )
+
+    def relay_copy(i, up):
+        which, cols = chunk(i)
+        to = 0 if up else 2
+        return pltpu.make_async_remote_copy(
+            src_ref=kv.at[which, to, :, cols], dst_ref=kv.at[which, to, :, cols],
+            send_sem=x_ssem.at[i, to // 2], recv_sem=f_rsem.at[i, to // 2],
+            device_id=opposite, device_id_type=MESH,
+        )
+
+    is_first, is_last = q == 0, q == 15
+
+    def relay(i):
+        for edge, up in ((is_first, True), (is_last, False)):
+
+            @pl.when(edge)
+            def _():
+                f_copy(i, up).wait_recv()
+                relay_copy(i, up).start()
+
+    for edge, to in ((is_first, 0), (is_last, 2)):
+
+        @pl.when(edge)
+        def _():
+            for which in (0, 1):
+                kv[which, to, :, pl.ds(KVC, KVC)] = jnp.zeros((FR, KVC), jnp.bfloat16)
+
+    def neighbours(act_up, act_down, up_edge, down_edge):
+        pl.when(jnp.logical_not(up_edge))(act_up)
+        pl.when(jnp.logical_not(down_edge))(act_down)
+
+    pl.semaphore_wait(barrier, 38)
+    for i in range(4):
+        k_copy(i).start()
+    for i in range(4):
+        k_copy(i).wait_recv()
+        neighbours(lambda: f_copy(i, True).start(), lambda: f_copy(i, False).start(), is_last, is_first)
+        if 1 <= i <= RELAYED:
+            relay(i - 1)
 
     w_swap = [
         pltpu.make_async_remote_copy(
@@ -202,6 +251,46 @@
     ]
     for cp in w_swap:
         cp.start()
+
+    for cp in inputs:
+        cp.wait()
+    first = first_ref[0, 0] - (q - 1) * FR
+    frame = lax.broadcasted_iota(jnp.int32, (WIN, 3 * FR), 1)
+    row = lax.broadcasted_iota(jnp.int32, (WIN, 3 * FR), 0)
+    band = jnp.where(frame == row + first, 1.0, 0.0).astype(jnp.bfloat16)
+    squares = jnp.zeros((TOK, DH), jnp.float32)
+    for part in (0, 1):
+        for i in (2 * part, 2 * part + 1):
+            neighbours(
+                lambda: f_copy(i, True).wait_recv(), lambda: f_copy(i, False).wait_recv(), is_first, is_last
+            )
+        part_cols = pl.ds(part * KVC, KVC)
+        keys, values = (
+            dot(band, kv[which, :, :, part_cols].reshape(3 * FR, KVC)).astype(jnp.bfloat16) for which in (0, 1)
+        )
+        for h in range(KV_HEADS // 2):
+            at = slice(h * DH, (h + 1) * DH)
+            heads = [pl.ds(((part * 4 + h) * GROUP + g) * DH, DH) for g in range(GROUP)]
+            rows = jnp.concatenate([queries_ref[:, cols] for cols in heads], axis=0)
+            scores = lax.dot_general(
+                rows, keys[:, at], (((1,), (1,)), ((), ())), preferred_element_type=jnp.float32
+            ) * (1.0 / math.sqrt(DH))
+            weights = jnp.exp(scores - jnp.max(scores, axis=1, keepdims=True))
+            total = jnp.sum(weights, axis=1, keepdims=True)
+            context = dot(weights.astype(jnp.bfloat16), values[:, at]) / total
+            for g, cols in enumerate(heads):
+                state = dec_ref[:, cols].astype(jnp.float32) + context[g * TOK : (g + 1) * TOK]
+                state_ref[:, cols] = state
+                squares += state * state
+    inverse = lax.rsqrt(jnp.sum(squares, axis=1, keepdims=True) * (1.0 / D) + 1e-06)
+    for h in range(HEADS):
+        cols = pl.ds(h * DH, DH)
+        normed_ref[:, cols] = (state_ref[:, cols] * inverse * gain_ref[:, cols]).astype(jnp.bfloat16)
+
+    outgoing(0)
+    each_peer(0, lambda d: a_copy(0, d).start())
+    self_a.start()
+    outgoing(1)
 
     own, mate = x * 2 + l, x * 2 + 1 - l
 
@@ -249,6 +338,8 @@
         if wave == 0:
             self_a.wait()
         each_peer(wave, lambda d: a_recv(wave, d).wait_recv())
+        if wave == 0:
+            each_peer(1, lambda d: a_copy(1, d).start())
         rows = dot(unpack_ref[...], in_msg[wave].reshape(PEERS * MSG, SEG)).astype(jnp.bfloat16)
         for g in range(SEGS):
             xg[wave, own, :, pl.ds(g * SEG, SEG)] = rows[g * HALF : (g + 1) * HALF]
@@ -394,14 +485,27 @@
         each_peer(wave, lambda d: b_recv(wave, d).wait_recv())
         fin[wave] = dot(unpack_ref[...], ret_in[wave].reshape(PEERS * MSG, SEG)).astype(jnp.bfloat16)
 
-    def partials(wave):
+    def partials(wave, send):
         partial(wave, PA)
-        s_start(wave, 0, 6, 3, 9)
+        if send:
+            s_start(wave, 0, 6, 3, 9)
         partial(wave, QA)
         partial(wave, QB)
-        s_start(wave, 13, 14, 15, 16)
+        if send:
+            s_start(wave, 13, 14, 15, 16)
         partial(wave, PB)
-        s_start(wave, 1, 7, 2, 8)
+        if send:
+            s_start(wave, 1, 7, 2, 8)
+
+    def add_back(wave):
+        for g in range(SEGS):
+            cols = pl.ds(g * SEG, SEG)
+            expert_out = dot(perm_t[:, wave * HALF : (wave + 1) * HALF], fin[wave, pl.ds(g * HALF, HALF)])
+            mixed = state_ref[:, cols] + scale * expert_out
+            if wave == 0:
+                state_ref[:, cols] = mixed
+            else:
+                out_ref[0, :, cols] = mixed.astype(jnp.bfloat16)
 
     arrive(0)
     gather_1(0)
@@ -416,34 +520,37 @@
         cp.wait_recv()
     hidden(0)
     gather_2(1)
-    partials(0)
+    partials(0, False)
     gather_3(1)
-    sum_qy(0)
-    sum_p2(0)
+    s_start(0, 0, 6, 3, 9, 13, 14, 15, 16, 1, 7, 2, 8)
     gather_4(1)
     hidden(1)
+    sum_p2(0)
+    sum_qy(0)
+    partials(1, True)
+    sum_p1(0)
     sum_q2(0)
-    sum_p1(0)
-    partials(1)
+    sum_p2(1)
+    sum_py(0)
     sum_q1(0)
-    sum_py(0)
     send_back(0)
     sum_qy(1)
-    sum_p2(1)
+    sum_p1(1)
     sum_q2(1)
-    sum_p1(1)
+    come_back(0)
+    add_back(0)
     sum_q1(1)
     sum_py(1)
     send_back(1)
-    come_back(0)
     come_back(1)
-
-    for g in range(SEGS):
-        cols = pl.ds(g * SEG, SEG)
-        rows = jnp.concatenate([fin[0, pl.ds(g * HALF, HALF)], fin[1, pl.ds(g * HALF, HALF)]], axis=0)
-        expert_out = dot(perm_t, rows)
-        out_ref[:, cols] = (state_ref[:, cols] + scale_ref[...] * expert_out).astype(jnp.bfloat16)
-
+    add_back(1)
+
+    for i in range(4):
+        k_copy(i).wait_send()
+        neighbours(lambda: f_copy(i, True).wait_send(), lambda: f_copy(i, False).wait_send(), is_last, is_first)
+        if i < RELAYED:
+            pl.when(is_first)(lambda: relay_copy(i, True).wait_send())
+            pl.when(is_last)(lambda: relay_copy(i, False).wait_send())
     for cp in w_swap:
         cp.wait_send()
     for wave in (0, 1):
@@ -455,17 +562,32 @@
             s_copy(wave, i).wait_send()
 
 
-def expert_layer(normed, state, ids, scale, w_in, w_out):
+def body(
+    queries, dec_state, enc_kv, band_start, norm_gain, route_ids, keep, route_prob, w_in, w_out
+):
     order = message_order()
     vmem = pl.BlockSpec(memory_space=pltpu.VMEM)
     hbm = pl.BlockSpec(memory_space=pl.ANY)
     bf = jnp.bfloat16
     return pl.pallas_call(
         moe_kernel,
-        out_shape=jax.ShapeDtypeStruct((TOK, D), bf),
-        in_specs=[vmem] * 7 + [hbm] * 2,
+        out_shape=jax.ShapeDtypeStruct((1, TOK, D), bf),
+        in_specs=[pl.BlockSpec(memory_space=pltpu.SMEM)] + [vmem] * 4 + [hbm] * 7,
         out_specs=vmem,
         scratch_shapes=[
+            pltpu.VMEM((SEGS * HALF, SEGS * HALF), bf),
+            pltpu.VMEM((SEGS * HALF, SEGS * HALF), bf),
+            pltpu.VMEM((TOK, D), bf),
+            pltpu.VMEM((TOK, D), bf),
+            pltpu.VMEM((TOK, D), jnp.float32),
+            pltpu.VMEM((TOK, D), bf),
+            pltpu.VMEM((2, 3, FR, KV_HEADS * DH), bf),
+            pltpu.SemaphoreType.DMA((4,)),
+            pltpu.SemaphoreType.DMA((4,)),
+            pltpu.SemaphoreType.DMA((4,)),
+            pltpu.SemaphoreType.DMA((4, 2)),
+            pltpu.SemaphoreType.DMA((4, 2)),
+            pltpu.SemaphoreType.DMA((2, 2)),
             pltpu.VMEM((2 * FS, D), bf),
             pltpu.VMEM((2 * FS, D), bf),
             pltpu.VMEM((8 * HALF, 2 * FS), bf),
@@ -503,35 +625,19 @@
             collective_id=0, has_side_effects=True, vmem_limit_bytes=60 * 2**20
         ),
     )(
+        band_start,
+        route_ids.reshape(1, TOK),
+        keep,
+        route_prob,
+        norm_gain.reshape(1, D),
         jnp.asarray(order, bf),
         jnp.asarray(order.T, bf),
-        normed,
-        state,
-        ids.reshape(TOK, 1),
-        ids.reshape(1, TOK),
-        scale.reshape(TOK, 1),
+        queries,
+        dec_state,
+        enc_kv,
         w_in,
         w_out,
     )
-
-
-def body(
-    queries, dec_state, enc_kv, band_start, norm_gain, route_ids, keep, route_prob, w_in, w_out
-):
-    own_pair = shifted(enc_kv[:, 0], "section", 1)
-    frames_dev = own_pair.shape[1]
-    offset = band_start[0, 0]
-    position = lax.axis_index("seq")
-    widened = extended(own_pair, (("seq", 1),), frames_dev)
-    local_first = offset - (position - 1) * frames_dev
-    band_pair = lax.dynamic_slice_in_dim(widened, local_first, WIN, 1)
-    context = cross_attend(queries[0], band_pair)
-    state = dec_state[0].astype(jnp.float32) + context
-    normed = (
-        state * lax.rsqrt(jnp.mean(state * state, axis=-1, keepdims=True) + 1e-06) * norm_gain
-    ).astype(jnp.bfloat16)
-    scale = keep[0].astype(jnp.float32) * route_prob[0]
-    return expert_layer(normed, state, route_ids[0], scale, w_in, w_out)[None]
 
 
 def solution(mesh):

time: 176 us -> 156 us (0.89)
  Pallas kernels: 132 us -> 153 us
  waiting for transfers between devices: 15.2 us -> 0 us
  local copies, waits for them, and re-layouts: 13 us -> 2.06 us
  starting transfers between devices: 7.55 us -> 0 us
  other arithmetic: 4.91 us -> 0 us
  matrix products: 3.03 us -> 0 us
    pallas_call x1, Pallas kernels: 132 us -> 153 us  [body(): pl.pallas_call(moe_kernel, out_shape=jax.ShapeDtypeStruct((1, TOK, D), bf...]
    ppermute x3 -> x0, waiting for transfers between devices: 15.2 us -> none  [the longest x1 7.85 us: shifted(): return lax.ppermute(block, axis, route)]
    ppermute x3 -> x0, starting transfers between devices: 7.55 us -> none  [the longest x1 3.57 us: extended(): lax.ppermute(tail, axis, [(i, (i + 1) % count) for i in range(ends)])]
    dot_general x2 -> x0, matrix products: 3.03 us -> none  [the longest x1 2.24 us: cross_attend(): jnp.einsum('kgtw,wkd->tkgd', rounded, values_b, preferred_element_type=jn...]
    another operation x1 -> x0, local copies, waits for them, and re-layouts: 2.99 us -> none  [cross_attend(): grouped = query_rows.reshape(tok_count, KV_HEADS, groups, DH)]
    convert_element_type x1 -> x0, other arithmetic: 2.8 us -> none  [body(): normed = (state * lax.rsqrt(jnp.mean(state * state, axis=-1, keepdims=Tru...]
    ppermute x3 -> x0, local copies, waits for them, and re-layouts: 2.39 us -> none  [the longest x1 1.41 us: extended(): lax.ppermute(head, axis, [((i + 1) % count, i) for i in range(ends)])]
    convert_element_type x1 -> x0, local copies, waits for them, and re-layouts: 2.32 us -> none  [body(): state = dec_state[0].astype(jnp.float32) + context]
  transfers between devices with their start and end apart: 3 -> 0, of which waited for: 3 -> 0; matrix products, arithmetic and copies ran while one was open for 4% -> 0% of each run, Pallas kernels for 0% -> 0%
where the time goes in v2:
time: 156 us
  Pallas kernels  153 us (98%)
  local copies, waits for them, and re-layouts  2.06 us (1%)
    pallas_call x1, Pallas kernels, body(): pl.pallas_call(moe_kernel, out_shape=jax.ShapeDtypeStruct((1, TOK, D), bf...  153 us

profile of v2, /device:TPU:1, one launch (start us, length us, event | category | flops | bytes accessed | tf_op | source)
XLA Modules:
  0.0 155.6 jit_solution(9010505655893563181)
XLA Ops:
  0.7 152.9 %shard_map.118 = bf16[1,96,4096]{2,1,0:T(8,128)(2,1)} custom-call(s32[1,1]{1,0:T(1,128)S(6)} %copy.14.first_ref, s32[1,96]{1,0:T(1,128)} %bitcast.3, s32[1,96]{1,0:T(1,128)} %keep_ref.1, f32[1,96]{1,0:T(1,128)} %prob_ref.1, f32[1,4096]{1,0:T(1,128)} %bitcast.2, bf16[384,384]{1,0:T(8,128)(2,1)} %constant.4.clone.unpack_hbm, ...), custom_call_target="tpu_custom_call" | custom-call | tf_op jit(solution)/shard_map/pallas_call | solution.py:572
  153.6 2.1 %copy.15 = bf16[1,96,4096]{2,1,0:T(8,128)(2,1)} copy(bf16[1,96,4096]{2,1,0:T(8,128)(2,1)} %shard_map.118) | data formatting | bytes 1572864

commit v3 on v2

--- a/solution.py
+++ b/solution.py
@@ -17,17 +17,19 @@
 
 TOK = 96
 HALF = 48
+SIDE = D // 2
 SEGS = 8
-SEG = D // SEGS
+SEG = SIDE // SEGS
 MSG = 24
 PEERS = 16
 FS = 320
-PA = (0, 1152)
-PB = (1152, 1152)
-QA = (2304, 896)
-QB = (3200, 896)
-PP = (0, 2304)
-QQ = (2304, 1792)
+UNITS = 4
+PA = (0, 640)
+PB = (640, 512)
+QA = (1152, 384)
+QB = (1536, 512)
+PP = (0, 1152)
+QQ = (1152, 896)
 FR = 160
 KVC = 512
 GROUP = HEADS // KV_HEADS
@@ -48,7 +50,7 @@
     out_ref,
     unpack_ref, pack_ref, queries_ref, dec_ref, state_ref, normed_ref, kv,
     in_sem, k_ssem, k_rsem, f_ssem, f_rsem, x_ssem,
-    win, wout, hid, xg, pt, out_msg, in_msg, ret_msg, ret_in, fin,
+    win, wout, acc, hid, xg, pt, out_msg, in_msg, ret_msg, ret_in,
     r_p2r, r_p2l, r_pr, r_pl, r_py, r_qy, r_q2r, r_q2l, r_qr, r_ql,
     w_sem, wx_ssem, wx_rsem, a_ssem, a_rsem, b_ssem, b_rsem, self_sem, g_ssem, g_rsem, s_ssem, s_rsem,
 ):
@@ -135,45 +137,51 @@
     def pack(rows):
         return dot(pack_ref[...], jnp.concatenate([rows[:, g * SEG : (g + 1) * SEG] for g in range(SEGS)], axis=0)).astype(jnp.bfloat16)
 
-    def a_copy(wave, d):
-        return pltpu.make_async_remote_copy(
-            src_ref=out_msg.at[wave, d], dst_ref=in_msg.at[wave, me],
-            send_sem=a_ssem.at[wave, d], recv_sem=a_rsem.at[wave, me],
-            device_id=peer(wave, d), device_id_type=MESH,
-        )
-
-    def a_recv(wave, d):
-        return pltpu.make_async_remote_copy(
-            src_ref=out_msg.at[wave, d], dst_ref=in_msg.at[wave, d],
-            send_sem=a_ssem.at[wave, d], recv_sem=a_rsem.at[wave, d],
-            device_id=peer(wave, d), device_id_type=MESH,
-        )
-
-    def b_copy(wave, d):
-        return pltpu.make_async_remote_copy(
-            src_ref=ret_msg.at[wave, d], dst_ref=ret_in.at[wave, me],
-            send_sem=b_ssem.at[wave, d], recv_sem=b_rsem.at[wave, me],
-            device_id=peer(wave, d), device_id_type=MESH,
-        )
-
-    def b_recv(wave, d):
-        return pltpu.make_async_remote_copy(
-            src_ref=ret_msg.at[wave, d], dst_ref=ret_in.at[wave, d],
-            send_sem=b_ssem.at[wave, d], recv_sem=b_rsem.at[wave, d],
-            device_id=peer(wave, d), device_id_type=MESH,
-        )
-
-    def each_peer(wave, act):
-        @pl.loop(1 if wave == 0 else 0, PEERS)
+    def a_copy(u, d):
+        return pltpu.make_async_remote_copy(
+            src_ref=out_msg.at[u, d], dst_ref=in_msg.at[u, me],
+            send_sem=a_ssem.at[u, d], recv_sem=a_rsem.at[u, me],
+            device_id=peer(u // 2, d), device_id_type=MESH,
+        )
+
+    def a_recv(u, d):
+        return pltpu.make_async_remote_copy(
+            src_ref=out_msg.at[u, d], dst_ref=in_msg.at[u, d],
+            send_sem=a_ssem.at[u, d], recv_sem=a_rsem.at[u, d],
+            device_id=peer(u // 2, d), device_id_type=MESH,
+        )
+
+    def b_copy(u, d):
+        return pltpu.make_async_remote_copy(
+            src_ref=ret_msg.at[u, d], dst_ref=ret_in.at[u, me],
+            send_sem=b_ssem.at[u, d], recv_sem=b_rsem.at[u, me],
+            device_id=peer(u // 2, d), device_id_type=MESH,
+        )
+
+    def b_recv(u, d):
+        return pltpu.make_async_remote_copy(
+            src_ref=ret_msg.at[u, d], dst_ref=ret_in.at[u, d],
+            send_sem=b_ssem.at[u, d], recv_sem=b_rsem.at[u, d],
+            device_id=peer(u // 2, d), device_id_type=MESH,
+        )
+
+    def each_peer(u, act):
+        @pl.loop(1 if u < 2 else 0, PEERS)
         def _(i):
             act((me + i) % PEERS)
 
-    self_a = pltpu.make_async_copy(out_msg.at[0, me], in_msg.at[0, me], self_sem.at[0])
-    self_b = pltpu.make_async_copy(ret_msg.at[0, me], ret_in.at[0, me], self_sem.at[1])
+    self_a = [pltpu.make_async_copy(out_msg.at[u, me], in_msg.at[u, me], self_sem.at[u]) for u in (0, 1)]
+    self_b = [pltpu.make_async_copy(ret_msg.at[u, me], ret_in.at[u, me], self_sem.at[2 + u]) for u in (0, 1)]
+
+    def a_start(u):
+        each_peer(u, lambda d: a_copy(u, d).start())
+        if u < 2:
+            self_a[u].start()
 
     def outgoing(wave):
         rows = dot(perm[wave * HALF : (wave + 1) * HALF], normed_ref[...]).astype(jnp.bfloat16)
-        out_msg[wave] = pack(rows).reshape(PEERS, MSG, SEG)
+        for side in (0, 1):
+            out_msg[2 * wave + side] = pack(rows[:, side * SIDE : (side + 1) * SIDE]).reshape(PEERS, MSG, SEG)
 
     nxt = ((s + 1) % 4, q, x)
 
@@ -288,9 +296,7 @@
         normed_ref[:, cols] = (state_ref[:, cols] * inverse * gain_ref[:, cols]).astype(jnp.bfloat16)
 
     outgoing(0)
-    each_peer(0, lambda d: a_copy(0, d).start())
-    self_a.start()
-    outgoing(1)
+    a_start(0)
 
     own, mate = x * 2 + l, x * 2 + 1 - l
 
@@ -318,11 +324,14 @@
         (blk(xo), QB, across, blk(xo, True)),
     ]
 
-    def g_copy(wave, i, received=False):
+    def wide(u, cols):
+        return pl.ds((u % 2) * SIDE + cols[0], cols[1])
+
+    def g_copy(u, i, received=False):
         sent, cols, there, got = gather[i]
-        ref = xg.at[wave, got if received else sent, :, pl.ds(*cols)]
-        return pltpu.make_async_remote_copy(
-            src_ref=ref, dst_ref=ref, send_sem=g_ssem.at[wave, i], recv_sem=g_rsem.at[wave, i],
+        ref = xg.at[u // 2, got if received else sent, :, wide(u, cols)]
+        return pltpu.make_async_remote_copy(
+            src_ref=ref, dst_ref=ref, send_sem=g_ssem.at[u, i], recv_sem=g_rsem.at[u, i],
             device_id=there, device_id_type=MESH,
         )
 
@@ -334,57 +343,51 @@
         for i in which:
             g_copy(wave, i, True).wait_recv()
 
-    def arrive(wave):
-        if wave == 0:
-            self_a.wait()
-        each_peer(wave, lambda d: a_recv(wave, d).wait_recv())
-        if wave == 0:
-            each_peer(1, lambda d: a_copy(1, d).start())
-        rows = dot(unpack_ref[...], in_msg[wave].reshape(PEERS * MSG, SEG)).astype(jnp.bfloat16)
+    def arrive(u):
+        if u < 2:
+            self_a[u].wait()
+        each_peer(u, lambda d: a_recv(u, d).wait_recv())
+        rows = dot(unpack_ref[...], in_msg[u].reshape(PEERS * MSG, SEG)).astype(jnp.bfloat16)
         for g in range(SEGS):
-            xg[wave, own, :, pl.ds(g * SEG, SEG)] = rows[g * HALF : (g + 1) * HALF]
+            xg[u // 2, own, :, wide(u, (g * SEG, SEG))] = rows[g * HALF : (g + 1) * HALF]
 
     def gather_1(wave):
         g_start(wave, 0, 1, 2, 3, 4, 5)
 
-    def gather_2(wave):
-        g_wait(wave, 0)
-        g_start(wave, 6, 7)
-        g_wait(wave, 1, 2)
-        g_start(wave, 8, 9, 10, 11)
-
-    def gather_3(wave):
-        g_wait(wave, 3, 4)
-        g_start(wave, 12, 13)
-        g_wait(wave, 6, 7)
-        g_start(wave, 14, 15)
-        g_wait(wave, 8, 9)
-        g_start(wave, 16, 17)
+    def hand_on(u, received, then):
+        g_wait(u, *received)
+        g_start(u, *then)
 
     def gather_4(wave):
         g_wait(wave, 5, 10, 11, 12, 13, 14, 15, 16, 17)
 
-    def hidden(wave):
-        rows = xg[wave].reshape(8 * HALF, D)
-        units = lax.dot_general(rows, win[...], (((1,), (1,)), ((), ())), preferred_element_type=jnp.float32)
-        hid[...] = jnp.maximum(units, 0.0).astype(jnp.bfloat16)
-
-    def partial(wave, cols):
-        part = dot(hid[...], wout[:, pl.ds(*cols)])
-        pt[wave, :, :, pl.ds(*cols)] = part.astype(jnp.bfloat16).reshape(8, HALF, cols[1])
+    def hidden(u):
+        rows = xg[u // 2, :, :, wide(u, (0, SIDE))].reshape(8 * HALF, SIDE)
+        units = lax.dot_general(
+            rows, win[:, wide(u, (0, SIDE))], (((1,), (1,)), ((), ())), preferred_element_type=jnp.float32
+        )
+        if u % 2 == 0:
+            acc[...] = units
+        else:
+            hid[...] = jnp.maximum(acc[...] + units, 0.0).astype(jnp.bfloat16)
+
+    def partial(u):
+        for cols in (PA, QQ, PB):
+            part = dot(hid[...], wout[:, wide(u, cols)])
+            pt[u // 2, :, :, wide(u, cols)] = part.astype(jnp.bfloat16).reshape(8, HALF, cols[1])
 
     def span(home, cols):
-        return lambda wave: pt.at[wave, home, :, pl.ds(*cols)]
+        return lambda u: pt.at[u // 2, home, :, wide(u, cols)]
 
     def inner(buf, i, cols):
-        return lambda wave: buf.at[wave, i, :, pl.ds(*cols)]
+        return lambda u: buf.at[u, i, :, pl.ds(*cols)]
 
     sums = []
     for f in (1, 0):
         far = f == 1
         sums += [
             (span(blk(xo, far), PA), inner(r_p2r, f, PA), left),
-            (span(blk(xo, far), PB), inner(r_p2l, f, PA), right),
+            (span(blk(xo, far), PB), inner(r_p2l, f, (0, PB[1])), right),
             (span(blk(xl, far), PB), inner(r_pr, f, PB), left),
             (span(blk(xr, far), PA), inner(r_pl, f, PA), right),
             (span(blk(xl, far), PA), inner(r_pr, f, PA), left),
@@ -398,7 +401,7 @@
         (span(blk(xr, True), QQ), inner(r_qy, 2, (0, QQ[1])), across),
         (span(mate, QQ), inner(r_qy, 3, (0, QQ[1])), across),
         (span(blk(xo), QA), inner(r_q2r, 0, q0), left),
-        (span(blk(xo), QB), inner(r_q2l, 0, q0), right),
+        (span(blk(xo), QB), inner(r_q2l, 0, (0, QB[1])), right),
         (span(blk(xl), QB), inner(r_qr, 0, q1), left),
         (span(blk(xr), QA), inner(r_ql, 0, q0), right),
         (span(blk(xl), QA), inner(r_qr, 0, q0), left),
@@ -420,130 +423,195 @@
         for i in which:
             s_copy(wave, i).wait_recv()
 
-    def add(wave, home, cols, *terms):
+    def add(u, home, cols, *terms):
         step = 128
 
         @pl.loop(0, cols[1] // step)
         def _(i):
-            here = pl.ds(pl.multiple_of(cols[0] + i * step, 128), step)
-            total = pt[wave, home, :, here].astype(jnp.float32)
-            for buf, j, first in terms:
-                total += buf[wave, j, :, pl.ds(pl.multiple_of(first + i * step, 128), step)].astype(jnp.float32)
-            pt[wave, home, :, here] = total.astype(jnp.bfloat16)
-
-    def sum_p2(wave):
-        for n, f in ((0, 1), (6, 0)):
-            far = f == 1
-            s_wait(wave, n, n + 1)
-            add(wave, blk(xl, far), PA, (r_p2r, f, 0))
-            s_start(wave, n + 4)
-            add(wave, blk(xr, far), PB, (r_p2l, f, 0))
-            s_start(wave, n + 5)
-
-    def sum_p1(wave):
-        for n, f in ((0, 1), (6, 0)):
-            s_wait(wave, n + 2, n + 3, n + 4, n + 5)
-            add(wave, blk(x, f == 1), PP, (r_pr, f, 0), (r_pl, f, 0))
-            if f == 1:
-                s_start(wave, 12)
-
-    def sum_py(wave):
-        s_wait(wave, 12)
-        add(wave, own, PP, (r_py, 0, 0))
-
-    def sum_qy(wave):
-        s_wait(wave, 13)
-        add(wave, blk(xo), QQ, (r_qy, 0, 0))
-        s_start(wave, 17, 18)
-        s_wait(wave, 14)
-        add(wave, blk(xl), QQ, (r_qy, 1, 0))
-        s_start(wave, 19)
-        s_wait(wave, 15)
-        add(wave, blk(xr), QQ, (r_qy, 2, 0))
-        s_start(wave, 20)
-
-    def sum_q2(wave):
-        s_wait(wave, 17, 18)
-        add(wave, blk(xl), QA, (r_q2r, 0, 0))
-        s_start(wave, 21)
-        add(wave, blk(xr), QB, (r_q2l, 0, 0))
-        s_start(wave, 22)
-
-    def sum_q1(wave):
-        s_wait(wave, 16, 19, 20, 21, 22)
-        add(wave, own, QQ, (r_qy, 3, 0), (r_qr, 0, 0), (r_ql, 0, 0))
-
-    def send_back(wave):
-        ret_msg[wave] = pack(pt[wave, own]).reshape(PEERS, MSG, SEG)
-        each_peer(wave, lambda d: b_copy(wave, d).start())
-        if wave == 0:
-            self_b.start()
-
-    def come_back(wave):
-        if wave == 0:
-            self_b.wait()
-        each_peer(wave, lambda d: b_recv(wave, d).wait_recv())
-        fin[wave] = dot(unpack_ref[...], ret_in[wave].reshape(PEERS * MSG, SEG)).astype(jnp.bfloat16)
-
-    def partials(wave, send):
-        partial(wave, PA)
-        if send:
-            s_start(wave, 0, 6, 3, 9)
-        partial(wave, QA)
-        partial(wave, QB)
-        if send:
-            s_start(wave, 13, 14, 15, 16)
-        partial(wave, PB)
-        if send:
-            s_start(wave, 1, 7, 2, 8)
-
-    def add_back(wave):
+            here = pl.ds(pl.multiple_of((u % 2) * SIDE + cols[0] + i * step, 128), step)
+            total = pt[u // 2, home, :, here].astype(jnp.float32)
+            for buf, j in terms:
+                total += buf[u, j, :, pl.ds(pl.multiple_of(i * step, 128), step)].astype(jnp.float32)
+            pt[u // 2, home, :, here] = total.astype(jnp.bfloat16)
+
+    def sum_p2(u, f):
+        n, far = (0, True) if f == 1 else (6, False)
+        s_wait(u, n, n + 1)
+        add(u, blk(xl, far), PA, (r_p2r, f))
+        s_start(u, n + 4)
+        add(u, blk(xr, far), PB, (r_p2l, f))
+        s_start(u, n + 5)
+
+    def sum_p1(u, f):
+        n, far = (0, True) if f == 1 else (6, False)
+        s_wait(u, n + 2, n + 3, n + 4, n + 5)
+        add(u, blk(x, far), PP, (r_pr, f), (r_pl, f))
+        if far:
+            s_start(u, 12)
+
+    def sum_py(u):
+        s_wait(u, 12)
+        add(u, own, PP, (r_py, 0))
+
+    def sum_qy(u, i):
+        s_wait(u, 13 + i)
+        add(u, blk((xo, xl, xr)[i]), QQ, (r_qy, i))
+        s_start(u, *((17, 18), (19,), (20,))[i])
+
+    def sum_q2(u):
+        s_wait(u, 17, 18)
+        add(u, blk(xl), QA, (r_q2r, 0))
+        s_start(u, 21)
+        add(u, blk(xr), QB, (r_q2l, 0))
+        s_start(u, 22)
+
+    def sum_q1(u):
+        s_wait(u, 16, 19, 20, 21, 22)
+        add(u, own, QQ, (r_qy, 3), (r_qr, 0), (r_ql, 0))
+
+    def send_back(u):
+        ret_msg[u] = pack(pt[u // 2, own, :, wide(u, (0, SIDE))]).reshape(PEERS, MSG, SEG)
+        each_peer(u, lambda d: b_copy(u, d).start())
+        if u < 2:
+            self_b[u].start()
+
+    def come_back(u):
+        if u < 2:
+            self_b[u].wait()
+        each_peer(u, lambda d: b_recv(u, d).wait_recv())
+        wave = u // 2
+        rows = dot(unpack_ref[...], ret_in[u].reshape(PEERS * MSG, SEG)).astype(jnp.bfloat16)
         for g in range(SEGS):
-            cols = pl.ds(g * SEG, SEG)
-            expert_out = dot(perm_t[:, wave * HALF : (wave + 1) * HALF], fin[wave, pl.ds(g * HALF, HALF)])
+            cols = wide(u, (g * SEG, SEG))
+            expert_out = dot(perm_t[:, wave * HALF : (wave + 1) * HALF], rows[g * HALF : (g + 1) * HALF])
             mixed = state_ref[:, cols] + scale * expert_out
             if wave == 0:
                 state_ref[:, cols] = mixed
             else:
                 out_ref[0, :, cols] = mixed.astype(jnp.bfloat16)
 
+    def sums_start(u):
+        s_start(u, 0, 6, 1, 7, 13, 14, 15, 16, 3, 9, 2, 8)
+
+    def sent(u, *kinds):
+        for kind in kinds:
+            if kind == "a":
+                each_peer(u, lambda d: a_recv(u, d).wait_send())
+            if kind == "g":
+                for i in range(len(gather)):
+                    g_copy(u, i).wait_send()
+            if kind == "s":
+                for i in range(len(sums)):
+                    s_copy(u, i).wait_send()
+            if kind == "b":
+                each_peer(u, lambda d: b_recv(u, d).wait_send())
+
+    a_start(1)
+    outgoing(1)
     arrive(0)
     gather_1(0)
-    gather_2(0)
+    a_start(2)
     arrive(1)
-    gather_3(0)
     gather_1(1)
+    hand_on(0, (1, 2), (8, 9, 10, 11))
+    a_start(3)
+    hand_on(0, (0,), (6, 7))
+    hand_on(0, (3, 4), (12, 13))
+    arrive(2)
+    hand_on(1, (0,), (6, 7))
+    hand_on(1, (1, 2), (8, 9, 10, 11))
+    gather_1(2)
+    hand_on(1, (3, 4), (12, 13))
+    hand_on(0, (8, 9), (16, 17))
+    arrive(3)
+    gather_1(3)
+    hand_on(0, (6, 7), (14, 15))
+    hand_on(1, (6, 7), (14, 15))
+    hand_on(1, (8, 9), (16, 17))
+    hand_on(2, (0,), (6, 7))
+    hand_on(2, (1, 2), (8, 9, 10, 11))
+    hand_on(2, (3, 4), (12, 13))
+    hand_on(3, (1, 2), (8, 9, 10, 11))
+    hand_on(3, (0,), (6, 7))
+    hand_on(3, (3, 4), (12, 13))
     gather_4(0)
     for cp in w_local:
         cp.wait()
     for cp in w_swap:
         cp.wait_recv()
     hidden(0)
-    gather_2(1)
-    partials(0, False)
-    gather_3(1)
-    s_start(0, 0, 6, 3, 9, 13, 14, 15, 16, 1, 7, 2, 8)
     gather_4(1)
     hidden(1)
-    sum_p2(0)
-    sum_qy(0)
-    partials(1, True)
-    sum_p1(0)
+    partial(1)
+    hand_on(2, (8, 9), (16, 17))
+    partial(0)
+    sums_start(0)
+    hand_on(3, (8, 9), (16, 17))
+    hand_on(2, (6, 7), (14, 15))
+    sums_start(1)
+    hand_on(3, (6, 7), (14, 15))
+    sum_p2(0, 1)
+    sum_qy(0, 0)
+    sum_p2(0, 0)
+    sum_qy(0, 1)
+    sum_qy(0, 2)
+    gather_4(2)
+    hidden(2)
+    sum_p2(1, 1)
+    sum_p2(1, 0)
+    sum_qy(1, 0)
+    gather_4(3)
+    hidden(3)
+    sum_p1(0, 1)
     sum_q2(0)
-    sum_p2(1)
+    partial(2)
+    sums_start(2)
+    sum_p1(0, 0)
+    sum_p1(1, 1)
+    partial(3)
+    sum_p1(1, 0)
     sum_py(0)
     sum_q1(0)
+    sum_qy(2, 0)
+    sum_p2(2, 1)
+    sums_start(3)
     send_back(0)
-    sum_qy(1)
-    sum_p1(1)
+    sent(0, "a", "g")
+    sum_qy(2, 2)
+    sum_qy(1, 1)
+    sum_qy(2, 1)
+    sum_qy(1, 2)
     sum_q2(1)
+    sum_q2(2)
+    sum_p2(2, 0)
+    sum_p1(2, 1)
+    sum_p2(3, 1)
+    sum_py(1)
+    sum_p2(3, 0)
     come_back(0)
-    add_back(0)
+    sum_qy(3, 0)
+    sum_qy(3, 1)
+    sum_qy(3, 2)
     sum_q1(1)
-    sum_py(1)
     send_back(1)
+    sum_q1(2)
+    sum_p1(2, 0)
+    sum_p1(3, 1)
+    sum_py(2)
+    send_back(2)
+    sum_q2(3)
+    sent(2, "a", "g")
+    sum_p1(3, 0)
+    sent(1, "a", "g")
+    sum_py(3)
+    sum_q1(3)
+    send_back(3)
+    sent(3, "a", "g")
     come_back(1)
-    add_back(1)
+    come_back(2)
+    come_back(3)
+    for u in range(UNITS):
+        sent(u, "s", "b")
 
     for i in range(4):
         k_copy(i).wait_send()
@@ -553,13 +621,6 @@
             pl.when(is_last)(lambda: relay_copy(i, False).wait_send())
     for cp in w_swap:
         cp.wait_send()
-    for wave in (0, 1):
-        each_peer(wave, lambda d: a_recv(wave, d).wait_send())
-        each_peer(wave, lambda d: b_recv(wave, d).wait_send())
-        for i in range(len(gather)):
-            g_copy(wave, i).wait_send()
-        for i in range(len(sums)):
-            s_copy(wave, i).wait_send()
 
 
 def body(
@@ -590,36 +651,36 @@
             pltpu.SemaphoreType.DMA((2, 2)),
             pltpu.VMEM((2 * FS, D), bf),
             pltpu.VMEM((2 * FS, D), bf),
+            pltpu.VMEM((8 * HALF, 2 * FS), jnp.float32),
             pltpu.VMEM((8 * HALF, 2 * FS), bf),
             pltpu.VMEM((2, 8, HALF, D), bf),
             pltpu.VMEM((2, 8, HALF, D), bf),
-            pltpu.VMEM((2, PEERS, MSG, SEG), bf),
-            pltpu.VMEM((2, PEERS, MSG, SEG), bf),
-            pltpu.VMEM((2, PEERS, MSG, SEG), bf),
-            pltpu.VMEM((2, PEERS, MSG, SEG), bf),
-            pltpu.VMEM((2, PEERS * MSG, SEG), bf),
-            pltpu.VMEM((2, 2, HALF, PA[1]), bf),
-            pltpu.VMEM((2, 2, HALF, PB[1]), bf),
-            pltpu.VMEM((2, 2, HALF, PP[1]), bf),
-            pltpu.VMEM((2, 2, HALF, PP[1]), bf),
-            pltpu.VMEM((2, 1, HALF, PP[1]), bf),
-            pltpu.VMEM((2, 4, HALF, QQ[1]), bf),
-            pltpu.VMEM((2, 1, HALF, QA[1]), bf),
-            pltpu.VMEM((2, 1, HALF, QB[1]), bf),
-            pltpu.VMEM((2, 1, HALF, QQ[1]), bf),
-            pltpu.VMEM((2, 1, HALF, QQ[1]), bf),
+            pltpu.VMEM((UNITS, PEERS, MSG, SEG), bf),
+            pltpu.VMEM((UNITS, PEERS, MSG, SEG), bf),
+            pltpu.VMEM((UNITS, PEERS, MSG, SEG), bf),
+            pltpu.VMEM((UNITS, PEERS, MSG, SEG), bf),
+            pltpu.VMEM((UNITS, 2, HALF, PA[1]), bf),
+            pltpu.VMEM((UNITS, 2, HALF, PB[1]), bf),
+            pltpu.VMEM((UNITS, 2, HALF, PP[1]), bf),
+            pltpu.VMEM((UNITS, 2, HALF, PP[1]), bf),
+            pltpu.VMEM((UNITS, 1, HALF, PP[1]), bf),
+            pltpu.VMEM((UNITS, 4, HALF, QQ[1]), bf),
+            pltpu.VMEM((UNITS, 1, HALF, QA[1]), bf),
+            pltpu.VMEM((UNITS, 1, HALF, QB[1]), bf),
+            pltpu.VMEM((UNITS, 1, HALF, QQ[1]), bf),
+            pltpu.VMEM((UNITS, 1, HALF, QQ[1]), bf),
             pltpu.SemaphoreType.DMA((2,)),
             pltpu.SemaphoreType.DMA((2,)),
             pltpu.SemaphoreType.DMA((2,)),
-            pltpu.SemaphoreType.DMA((2, PEERS)),
-            pltpu.SemaphoreType.DMA((2, PEERS)),
-            pltpu.SemaphoreType.DMA((2, PEERS)),
-            pltpu.SemaphoreType.DMA((2, PEERS)),
-            pltpu.SemaphoreType.DMA((2,)),
-            pltpu.SemaphoreType.DMA((2, 18)),
-            pltpu.SemaphoreType.DMA((2, 18)),
-            pltpu.SemaphoreType.DMA((2, 23)),
-            pltpu.SemaphoreType.DMA((2, 23)),
+            pltpu.SemaphoreType.DMA((UNITS, PEERS)),
+            pltpu.SemaphoreType.DMA((UNITS, PEERS)),
+            pltpu.SemaphoreType.DMA((UNITS, PEERS)),
+            pltpu.SemaphoreType.DMA((UNITS, PEERS)),
+            pltpu.SemaphoreType.DMA((4,)),
+            pltpu.SemaphoreType.DMA((UNITS, 18)),
+            pltpu.SemaphoreType.DMA((UNITS, 18)),
+            pltpu.SemaphoreType.DMA((UNITS, 23)),
+            pltpu.SemaphoreType.DMA((UNITS, 23)),
         ],
         compiler_params=pltpu.CompilerParams(
             collective_id=0, has_side_effects=True, vmem_limit_bytes=60 * 2**20

time: 156 us -> 149 us (0.955)
  Pallas kernels: 153 us -> 146 us
    pallas_call x1, Pallas kernels: 153 us -> 146 us  [body(): pl.pallas_call(moe_kernel, out_shape=jax.ShapeDtypeStruct((1, TOK, D), bf...]
where the time goes in v3:
time: 149 us
  Pallas kernels  146 us (98%)
  local copies, waits for them, and re-layouts  2.06 us (1%)
    pallas_call x1, Pallas kernels, body(): pl.pallas_call(moe_kernel, out_shape=jax.ShapeDtypeStruct((1, TOK, D), bf...  146 us

profile of v3, /device:TPU:1, one launch (start us, length us, event | category | flops | bytes accessed | tf_op | source)
XLA Modules:
  0.0 148.9 jit_solution(3528383152474163699)
XLA Ops:
  0.7 146.2 %shard_map.118 = bf16[1,96,4096]{2,1,0:T(8,128)(2,1)} custom-call(s32[1,1]{1,0:T(1,128)S(6)} %copy.14.first_ref, s32[1,96]{1,0:T(1,128)} %bitcast.3, s32[1,96]{1,0:T(1,128)} %keep_ref.1, f32[1,96]{1,0:T(1,128)} %prob_ref.1, f32[1,4096]{1,0:T(1,128)} %bitcast.2, bf16[384,384]{1,0:T(8,128)(2,1)} %constant.4.clone.unpack_hbm, ...), custom_call_target="tpu_custom_call" | custom-call | tf_op jit(solution)/shard_map/pallas_call | solution.py:633
  146.8 2.1 %copy.15 = bf16[1,96,4096]{2,1,0:T(8,128)(2,1)} copy(bf16[1,96,4096]{2,1,0:T(8,128)(2,1)} %shard_map.118) | data formatting | bytes 1572864

commit v4 on v3

--- a/solution.py
+++ b/solution.py
@@ -513,101 +513,101 @@
     a_start(2)
     arrive(1)
     gather_1(1)
-    hand_on(0, (1, 2), (8, 9, 10, 11))
     a_start(3)
     hand_on(0, (0,), (6, 7))
+    hand_on(0, (1, 2), (8, 9, 10, 11))
     hand_on(0, (3, 4), (12, 13))
     arrive(2)
+    gather_1(2)
     hand_on(1, (0,), (6, 7))
     hand_on(1, (1, 2), (8, 9, 10, 11))
-    gather_1(2)
     hand_on(1, (3, 4), (12, 13))
+    arrive(3)
+    hand_on(0, (6, 7), (14, 15))
+    gather_1(3)
     hand_on(0, (8, 9), (16, 17))
-    arrive(3)
-    gather_1(3)
-    hand_on(0, (6, 7), (14, 15))
-    hand_on(1, (6, 7), (14, 15))
-    hand_on(1, (8, 9), (16, 17))
     hand_on(2, (0,), (6, 7))
     hand_on(2, (1, 2), (8, 9, 10, 11))
     hand_on(2, (3, 4), (12, 13))
+    hand_on(1, (6, 7), (14, 15))
+    hand_on(1, (8, 9), (16, 17))
+    hand_on(3, (0,), (6, 7))
     hand_on(3, (1, 2), (8, 9, 10, 11))
-    hand_on(3, (0,), (6, 7))
-    hand_on(3, (3, 4), (12, 13))
     gather_4(0)
     for cp in w_local:
         cp.wait()
     for cp in w_swap:
         cp.wait_recv()
     hidden(0)
+    hand_on(3, (3, 4), (12, 13))
+    hand_on(2, (6, 7), (14, 15))
+    hand_on(2, (8, 9), (16, 17))
     gather_4(1)
     hidden(1)
-    partial(1)
-    hand_on(2, (8, 9), (16, 17))
     partial(0)
     sums_start(0)
+    hand_on(3, (6, 7), (14, 15))
+    partial(1)
     hand_on(3, (8, 9), (16, 17))
-    hand_on(2, (6, 7), (14, 15))
     sums_start(1)
-    hand_on(3, (6, 7), (14, 15))
+    gather_4(2)
+    hidden(2)
+    sum_qy(0, 0)
     sum_p2(0, 1)
-    sum_qy(0, 0)
     sum_p2(0, 0)
     sum_qy(0, 1)
     sum_qy(0, 2)
-    gather_4(2)
-    hidden(2)
     sum_p2(1, 1)
     sum_p2(1, 0)
-    sum_qy(1, 0)
     gather_4(3)
     hidden(3)
+    partial(3)
+    sum_q2(0)
+    sum_qy(1, 0)
     sum_p1(0, 1)
-    sum_q2(0)
     partial(2)
     sums_start(2)
+    sum_qy(1, 2)
+    sum_qy(1, 1)
+    sum_p1(1, 1)
     sum_p1(0, 0)
-    sum_p1(1, 1)
-    partial(3)
     sum_p1(1, 0)
+    sum_q1(0)
     sum_py(0)
-    sum_q1(0)
+    send_back(0)
+    sum_p2(2, 1)
     sum_qy(2, 0)
-    sum_p2(2, 1)
+    sum_q2(1)
     sums_start(3)
-    send_back(0)
+    sum_qy(2, 1)
+    sum_p2(2, 0)
     sent(0, "a", "g")
     sum_qy(2, 2)
-    sum_qy(1, 1)
-    sum_qy(2, 1)
-    sum_qy(1, 2)
-    sum_q2(1)
+    sum_p1(2, 1)
     sum_q2(2)
-    sum_p2(2, 0)
-    sum_p1(2, 1)
+    come_back(0)
+    sum_py(1)
     sum_p2(3, 1)
-    sum_py(1)
+    sum_q1(1)
+    sum_qy(3, 0)
+    send_back(1)
+    sum_qy(3, 1)
+    sent(1, "a", "g")
     sum_p2(3, 0)
-    come_back(0)
-    sum_qy(3, 0)
-    sum_qy(3, 1)
     sum_qy(3, 2)
-    sum_q1(1)
-    send_back(1)
+    sum_p1(2, 0)
     sum_q1(2)
-    sum_p1(2, 0)
     sum_p1(3, 1)
+    sum_q2(3)
     sum_py(2)
     send_back(2)
-    sum_q2(3)
+    sum_p1(3, 0)
     sent(2, "a", "g")
-    sum_p1(3, 0)
-    sent(1, "a", "g")
     sum_py(3)
     sum_q1(3)
     send_back(3)
+    come_back(1)
     sent(3, "a", "g")
-    come_back(1)
     come_back(2)
     come_back(3)
     for u in range(UNITS):

time: 149 us -> 150 us (level)
  no operation moved by 1% of the time
where the time goes in v4:
time: 150 us
  Pallas kernels  147 us (98%)
  local copies, waits for them, and re-layouts  2.06 us (1%)
    pallas_call x1, Pallas kernels, body(): pl.pallas_call(moe_kernel, out_shape=jax.ShapeDtypeStruct((1, TOK, D), bf...  147 us

profile of v4, /device:TPU:1, one launch (start us, length us, event | category | flops | bytes accessed | tf_op | source)
XLA Modules:
  0.0 149.7 jit_solution(15886494742731655503)
XLA Ops:
  0.7 147.0 %shard_map.118 = bf16[1,96,4096]{2,1,0:T(8,128)(2,1)} custom-call(s32[1,1]{1,0:T(1,128)S(6)} %copy.14.first_ref, s32[1,96]{1,0:T(1,128)} %bitcast.3, s32[1,96]{1,0:T(1,128)} %keep_ref.1, f32[1,96]{1,0:T(1,128)} %prob_ref.1, f32[1,4096]{1,0:T(1,128)} %bitcast.2, bf16[384,384]{1,0:T(8,128)(2,1)} %constant.4.clone.unpack_hbm, ...), custom_call_target="tpu_custom_call" | custom-call | tf_op jit(solution)/shard_map/pallas_call | solution.py:633
  147.6 2.1 %copy.15 = bf16[1,96,4096]{2,1,0:T(8,128)(2,1)} copy(bf16[1,96,4096]{2,1,0:T(8,128)(2,1)} %shard_map.118) | data formatting | bytes 1572864
